TPU v7x, 32 devices: a whole 2x2x4 slice. The times are simulated.
32 devices in a mesh: rep: 8 (over y, x, core), shard: 4 (over z).
Axes of the slice: x: 2, y: 2, z: 4, core: 2. Of those that a mesh axis runs over, the one named last changes fastest.
Arguments:
- hidden_in: float32 [32768, 768], P(('rep', 'shard')), may hold values from -6 to 6
- cotangent: float32 [32768, 768], P(('rep', 'shard')), may hold values from -6 to 6
- seg_ids: int32 [32768], P(('rep', 'shard')), may hold values from 0 to 127, as said below
- first_gain: bfloat16 [768], P('shard'), may hold values from 0.5 to 1.5
- first_shift: bfloat16 [768], P('shard'), may hold values from -1 to 1
- second_gain: bfloat16 [768], P('shard'), may hold values from 0.5 to 1.5
- second_shift: bfloat16 [768], P('shard'), may hold values from -1 to 1
- qkv_weight: bfloat16 [768, 2304], P('shard'), may hold values from -0.21875 to 0.21875
- qkv_bias: bfloat16 [2304], P('shard'), may hold values from -1.5 to 1.5
- out_weight: bfloat16 [768, 768], P('shard'), may hold values from -1.25 to 1.25
- out_bias: bfloat16 [768], P('shard'), may hold values from -1.5 to 1.5
- up_weight: bfloat16 [768, 3072], P('shard'), may hold values from -0.21875 to 0.21875
- up_bias: bfloat16 [3072], P('shard'), may hold values from -1.5 to 1.5
- down_weight: bfloat16 [3072, 768], P('shard'), may hold values from -0.109375 to 0.109375
- down_bias: bfloat16 [768], P('shard'), may hold values from -1.5 to 1.5
Outputs:
- output: float32 [32768, 768], P(('rep', 'shard'))
- input_grad: float32 [32768, 768], P(('rep', 'shard'))
- first_gain_grad: float32 [768], P('shard')
- first_shift_grad: float32 [768], P('shard')
- second_gain_grad: float32 [768], P('shard')
- second_shift_grad: float32 [768], P('shard')
- qkv_weight_grad: float32 [768, 2304], P('shard')
- qkv_bias_grad: float32 [2304], P('shard')
- out_weight_grad: float32 [768, 768], P('shard')
- out_bias_grad: float32 [768], P('shard')
- up_weight_grad: float32 [768, 3072], P('shard')
- up_bias_grad: float32 [3072], P('shard')
- down_weight_grad: float32 [3072, 768], P('shard')
- down_bias_grad: float32 [768], P('shard')
Inputs may be any that keep to these rules, and one draw needn't show every extreme that they name: Within each aligned block of 1024 rows (one device's token slots) seg_ids start at 0 on the block's first row, never fall, rise by at most one from row to row and only on rows whose place in the block is a multiple of 8; every slot belongs to a sequence; in every draw some block holds one single sequence of 1024 tokens, and another holds 128 sequences of 8 tokens.
All inputs are finite; a program needn't handle non-finite values.
Results may differ from a plain program's by a relative error of at most 0.0091.
Values may be sent and summed in bfloat16 or wider, within the bound.
No kernel may reach another device: no remote copies, remote signals or barrier semaphores. Data moves between devices by JAX's collectives and lax.ppermute only.
A program may use at most 320 MiB of HBM per device.

v0:
```python
import jax
import jax.numpy as jnp
from jax import lax
from jax.sharding import PartitionSpec as P

D = 768
H = 12
HD = 64
ROT = 16


norm_eps = 1e-05


def layer_norm(values, gain, shift):
    centre = values - jnp.mean(values, axis=-1, keepdims=True)
    spread = jnp.mean(centre * centre, axis=-1, keepdims=True)
    return centre * lax.rsqrt(spread + norm_eps) * gain + shift


def seq_positions(segments):
    row_index = jnp.arange(segments.shape[0], dtype=jnp.int32)
    previous = jnp.concatenate([jnp.full((1,), -1, jnp.int32), segments[:-1]])
    starts = jnp.where(segments != previous, row_index, 0)
    return row_index - lax.cummax(starts, axis=0)


def rotate(heads_in, places):
    half = ROT // 2
    freqs = 1.0 / 10000.0 ** (jnp.arange(half, dtype=jnp.float32) * 2.0 / ROT)
    angles = places.astype(jnp.float32)[:, None] * freqs[None, :]
    cosine = jnp.cos(angles)[:, None, :]
    sine = jnp.sin(angles)[:, None, :]
    first = heads_in[..., :half]
    second = heads_in[..., half:ROT]
    return jnp.concatenate(
        [first * cosine - second * sine, second * cosine + first * sine, heads_in[..., ROT:]],
        axis=-1,
    )


def gelu_exact(values):
    return jax.nn.gelu(values, approximate=False)


def block_scores(query_b, key_b, segments, first_row, block_rows, score_scale):
    q_block = query_b[first_row : first_row + block_rows]
    raw_scores = (
        jnp.einsum("qhd,khd->hqk", q_block, key_b, preferred_element_type=jnp.float32) * score_scale
    )
    row_index = jnp.arange(segments.shape[0], dtype=jnp.int32)
    rows_here = row_index[first_row : first_row + block_rows]
    seg_here = segments[first_row : first_row + block_rows]
    allowed = (seg_here[:, None] == segments[None, :]) & (row_index[None, :] <= rows_here[:, None])
    return (jnp.where(allowed[None], raw_scores, -1e30), q_block)


def body(
    hidden_in,
    cotangent,
    seg_ids,
    first_gain,
    first_shift,
    second_gain,
    second_shift,
    qkv_weight,
    qkv_bias,
    out_weight,
    out_bias,
    up_weight,
    up_bias,
    down_weight,
    down_bias,
):
    gathered = (
        lax.all_gather(first_gain, "shard", axis=0, tiled=True),
        lax.all_gather(first_shift, "shard", axis=0, tiled=True),
        lax.all_gather(second_gain, "shard", axis=0, tiled=True),
        lax.all_gather(second_shift, "shard", axis=0, tiled=True),
        lax.all_gather(qkv_weight, "shard", axis=0, tiled=True),
        lax.all_gather(qkv_bias, "shard", axis=0, tiled=True),
        lax.all_gather(out_weight, "shard", axis=0, tiled=True),
        lax.all_gather(out_bias, "shard", axis=0, tiled=True),
        lax.all_gather(up_weight, "shard", axis=0, tiled=True),
        lax.all_gather(up_bias, "shard", axis=0, tiled=True),
        lax.all_gather(down_weight, "shard", axis=0, tiled=True),
        lax.all_gather(down_bias, "shard", axis=0, tiled=True),
    )
    tokens_here = hidden_in.shape[0]
    score_scale = HD ** (-0.5)
    block_rows = min(512, tokens_here)
    places = seq_positions(seg_ids)
    first_normed, pull_first = jax.vjp(
        layer_norm, hidden_in, gathered[0].astype(jnp.float32), gathered[1].astype(jnp.float32)
    )
    first_b = first_normed.astype(jnp.bfloat16)
    qkv = jnp.dot(first_b, gathered[4], preferred_element_type=jnp.float32) + gathered[5].astype(
        jnp.float32
    )
    qkv = qkv.reshape(tokens_here, 3, H, HD)

    def rotate_pair(query_in, key_in):
        return (rotate(query_in, places), rotate(key_in, places))

    rotated, pull_rotate = jax.vjp(rotate_pair, qkv[:, 0], qkv[:, 1])
    query_b = rotated[0].astype(jnp.bfloat16)
    key_b = rotated[1].astype(jnp.bfloat16)
    value_b = qkv[:, 2].astype(jnp.bfloat16)
    mixed_parts = []
    logsum_parts = []
    for first_row in range(0, tokens_here, block_rows):
        masked, q_block = block_scores(query_b, key_b, seg_ids, first_row, block_rows, score_scale)
        highest_score = jnp.max(masked, axis=-1, keepdims=True)
        expo_scores = jnp.exp(masked - highest_score)
        total = jnp.sum(expo_scores, axis=-1, keepdims=True)
        probs = expo_scores / total
        logsum_parts.append(highest_score + jnp.log(total))
        mixed_parts.append(
            jnp.einsum(
                "hqk,khd->qhd",
                probs.astype(jnp.bfloat16),
                value_b,
                preferred_element_type=jnp.float32,
            )
        )
    mixed_b = jnp.concatenate(mixed_parts, axis=0).astype(jnp.bfloat16).reshape(tokens_here, D)
    attn_out = jnp.dot(mixed_b, gathered[6], preferred_element_type=jnp.float32) + gathered[
        7
    ].astype(jnp.float32)
    second_normed, pull_second = jax.vjp(
        layer_norm, hidden_in, gathered[2].astype(jnp.float32), gathered[3].astype(jnp.float32)
    )
    second_b = second_normed.astype(jnp.bfloat16)
    up_vals = jnp.dot(second_b, gathered[8], preferred_element_type=jnp.float32) + gathered[
        9
    ].astype(jnp.float32)
    act_vals, pull_gelu = jax.vjp(gelu_exact, up_vals)
    act_b = act_vals.astype(jnp.bfloat16)
    mlp_out = jnp.dot(act_b, gathered[10], preferred_element_type=jnp.float32) + gathered[
        11
    ].astype(jnp.float32)
    output = hidden_in + attn_out + mlp_out
    back_weights = (
        lax.all_gather(first_gain, "shard", axis=0, tiled=True),
        lax.all_gather(first_shift, "shard", axis=0, tiled=True),
        lax.all_gather(second_gain, "shard", axis=0, tiled=True),
        lax.all_gather(second_shift, "shard", axis=0, tiled=True),
        lax.all_gather(qkv_weight, "shard", axis=0, tiled=True),
        lax.all_gather(qkv_bias, "shard", axis=0, tiled=True),
        lax.all_gather(out_weight, "shard", axis=0, tiled=True),
        lax.all_gather(out_bias, "shard", axis=0, tiled=True),
        lax.all_gather(up_weight, "shard", axis=0, tiled=True),
        lax.all_gather(up_bias, "shard", axis=0, tiled=True),
        lax.all_gather(down_weight, "shard", axis=0, tiled=True),
        lax.all_gather(down_bias, "shard", axis=0, tiled=True),
    )
    cot_b = cotangent.astype(jnp.bfloat16)
    bias_out_g = jnp.sum(cotangent, axis=0)
    out_weight_g = jnp.einsum("td,te->de", mixed_b, cot_b, preferred_element_type=jnp.float32)
    down_weight_g = jnp.einsum("tf,te->fe", act_b, cot_b, preferred_element_type=jnp.float32)
    act_grad = jnp.einsum("te,fe->tf", cot_b, back_weights[10], preferred_element_type=jnp.float32)
    up_grad_b = pull_gelu(act_grad)[0].astype(jnp.bfloat16)
    up_bias_g = jnp.sum(up_grad_b.astype(jnp.float32), axis=0)
    up_weight_g = jnp.einsum("td,tf->df", second_b, up_grad_b, preferred_element_type=jnp.float32)
    second_in_grad = jnp.einsum(
        "tf,df->td", up_grad_b, back_weights[8], preferred_element_type=jnp.float32
    )
    second_x_grad, second_gain_g, second_shift_g = pull_second(second_in_grad)
    mixed_grad_b = (
        jnp.einsum("te,de->td", cot_b, back_weights[6], preferred_element_type=jnp.float32)
        .astype(jnp.bfloat16)
        .reshape(tokens_here, H, HD)
    )
    query_parts = []
    key_grad = jnp.zeros((tokens_here, H, HD), jnp.float32)
    value_grad = jnp.zeros((tokens_here, H, HD), jnp.float32)
    for block_number, first_row in enumerate(range(0, tokens_here, block_rows)):
        masked, q_block = block_scores(query_b, key_b, seg_ids, first_row, block_rows, score_scale)
        probs = jnp.exp(masked - logsum_parts[block_number])
        grad_block = mixed_grad_b[first_row : first_row + block_rows]
        probs_grad = jnp.einsum(
            "qhd,khd->hqk", grad_block, value_b, preferred_element_type=jnp.float32
        )
        value_grad = value_grad + jnp.einsum(
            "hqk,qhd->khd",
            probs.astype(jnp.bfloat16),
            grad_block,
            preferred_element_type=jnp.float32,
        )
        scores_grad = (
            probs * (probs_grad - jnp.sum(probs_grad * probs, axis=-1, keepdims=True))
        ).astype(jnp.bfloat16)
        query_parts.append(
            jnp.einsum("hqk,khd->qhd", scores_grad, key_b, preferred_element_type=jnp.float32)
            * score_scale
        )
        key_grad = (
            key_grad
            + jnp.einsum("hqk,qhd->khd", scores_grad, q_block, preferred_element_type=jnp.float32)
            * score_scale
        )
    query_grad = jnp.concatenate(query_parts, axis=0)
    query_in_grad, key_in_grad = pull_rotate((query_grad, key_grad))
    qkv_grad_b = (
        jnp.stack([query_in_grad, key_in_grad, value_grad], axis=1)
        .reshape(tokens_here, 3 * D)
        .astype(jnp.bfloat16)
    )
    qkv_bias_g = jnp.sum(qkv_grad_b.astype(jnp.float32), axis=0)
    qkv_weight_g = jnp.einsum("td,te->de", first_b, qkv_grad_b, preferred_element_type=jnp.float32)
    first_in_grad = jnp.einsum(
        "te,de->td", qkv_grad_b, back_weights[4], preferred_element_type=jnp.float32
    )
    first_x_grad, first_gain_g, first_shift_g = pull_first(first_in_grad)
    input_grad = cotangent + first_x_grad + second_x_grad
    all_owned = (
        lax.psum_scatter(first_gain_g, "shard", scatter_dimension=0, tiled=True),
        lax.psum_scatter(first_shift_g, "shard", scatter_dimension=0, tiled=True),
        lax.psum_scatter(second_gain_g, "shard", scatter_dimension=0, tiled=True),
        lax.psum_scatter(second_shift_g, "shard", scatter_dimension=0, tiled=True),
        lax.psum_scatter(qkv_weight_g, "shard", scatter_dimension=0, tiled=True),
        lax.psum_scatter(qkv_bias_g, "shard", scatter_dimension=0, tiled=True),
        lax.psum_scatter(out_weight_g, "shard", scatter_dimension=0, tiled=True),
        lax.psum_scatter(bias_out_g, "shard", scatter_dimension=0, tiled=True),
        lax.psum_scatter(up_weight_g, "shard", scatter_dimension=0, tiled=True),
        lax.psum_scatter(up_bias_g, "shard", scatter_dimension=0, tiled=True),
        lax.psum_scatter(down_weight_g, "shard", scatter_dimension=0, tiled=True),
        lax.psum_scatter(bias_out_g, "shard", scatter_dimension=0, tiled=True),
    )
    summed = lax.psum(
        (
            all_owned[0],
            all_owned[1],
            all_owned[2],
            all_owned[3],
            all_owned[4],
            all_owned[5],
            all_owned[6],
            all_owned[7],
            all_owned[8],
            all_owned[9],
            all_owned[10],
            all_owned[11],
        ),
        "rep",
    )
    return (
        output,
        input_grad,
        summed[0],
        summed[1],
        summed[2],
        summed[3],
        summed[4],
        summed[5],
        summed[6],
        summed[7],
        summed[8],
        summed[9],
        summed[10],
        summed[11],
    )


def solution(mesh):
    in_specs = (
        P(("rep", "shard"), None),
        P(("rep", "shard"), None),
        P(("rep", "shard")),
        P("shard"),
        P("shard"),
        P("shard"),
        P("shard"),
        P("shard", None),
        P("shard"),
        P("shard", None),
        P("shard"),
        P("shard", None),
        P("shard"),
        P("shard", None),
        P("shard"),
    )
    out_specs = (
        P(("rep", "shard"), None),
        P(("rep", "shard"), None),
        P("shard"),
        P("shard"),
        P("shard"),
        P("shard"),
        P("shard", None),
        P("shard"),
        P("shard", None),
        P("shard"),
        P("shard", None),
        P("shard"),
        P("shard", None),
        P("shard"),
    )
    return jax.shard_map(body, mesh=mesh, in_specs=in_specs, out_specs=out_specs, check_vma=False)
```

profile of v0, /device:TPU:0, one launch (start us, length us, event | category | flops | bytes accessed | tf_op | source)
XLA Modules:
  0.0 964.7 jit_solution(9652521078231420030)
XLA Ops:
  13.8 22.7 %all-reduce.23 = (bf16[768]{0:T(1024)(128)(2,1)}, bf16[768]{0:T(1024)(128)(2,1)}, bf16[768]{0:T(1024)(128)(2,1)}, bf16[768]{0:T(1024)(128)(2,1)}, bf16[2304]{0:T...) all-reduce(bf16[768]{0:T(1024)(128)(2,1)S(1)} %dynamic-update-slice, ...), channel_id=1, replica_groups=mesh['rep'=8,'shard'=4] {'shard'}, use_global_device_ids=true, to_apply=%add.11 | all-reduce | flops 6912 | bytes 27648
  38.5 4.9 fusion.55
  43.6 2.0 fusion.21
  45.5 3.2 convolution_convert_fusion
  50.0 64.5 %all-gather.6.cloned.1.call-done = bf16[768,2304]{1,0:T(8,128)(2,1)} async-done(((bf16[192,2304]{1,0:T(8,128)(2,1)}), bf16[768,2304]{1,0:T(8,128)(2,1)}) %all-gather.6.cloned.1.call-update) | async-done | bytes 3538960 | tf_op jit(solution)/shard_map/all_gather | solution.py:80
  114.5 8.6 convolution_add_fusion
  123.1 9.7 %copy.33 = f32[1024,2304]{0,1:T(8,128)} copy(f32[1024,2304]{1,0:T(8,128)} %convolution_add_fusion) | data formatting | bytes 18874368 | tf_op jit(solution)/shard_map/add | solution.py:97
  132.8 3.4 slice_bitcast_fusion
  137.4 11.0 %fusion.18 = (f32[12,512]{1,0:T(8,128)S(1)}, f32[12,512,1024]{2,1,0:T(8,128)}) fusion(pred[512,1024]{1,0:T(8,128)(4,1)S(1)} %copy-done.8, bf16[1024,12,48]{0,2,1:T(8,128)(2,1)S(1)} %slice.136, bf16[1024,12,8]{0,2,1:T(8,128)(2,1)S(1)} %get-tuple-element.62, bf16[1024,12,8]{0,2,1:T(8,128)(2,1)S(1)} %get-tuple-element.61, ...), kind=kOutput, calls=%fused_computation.42 | convolution fusion | flops 828893184 | bytes 28073984 | tf_op jit(solution)/shard_map/qhd,khd->hqk/dot_general | solution.py:49
  148.4 11.9 %fusion = f32[12,512]{1,0:T(8,128)S(1)} fusion(f32[12,512]{1,0:T(8,128)S(1)} %get-tuple-element.87, f32[12,512,1024]{2,1,0:T(8,128)} %get-tuple-element.88, pred[512,1024]{1,0:T(8,128)(4,1)S(1)} %copy-done.8), kind=kLoop, calls=%fused_computation.12 | loop fusion | flops 25159680 | bytes 25739264 | tf_op jit(solution)/shard_map/reduce_sum | solution.py:115
  160.4 11.2 %fusion.19 = (f32[12,512]{1,0:T(8,128)S(1)}, f32[12,512,1024]{2,1,0:T(8,128)}) fusion(pred[512,1024]{1,0:T(8,128)(4,1)S(1)} %copy-done.9, bf16[1024,12,48]{0,2,1:T(8,128)(2,1)S(1)} %slice.136, bf16[1024,12,8]{0,2,1:T(8,128)(2,1)S(1)} %get-tuple-element.62, bf16[1024,12,8]{0,2,1:T(8,128)(2,1)S(1)} %get-tuple-element.61, ...), kind=kOutput, calls=%fused_computation.43 | convolution fusion | flops 828893184 | bytes 28073984 | tf_op jit(solution)/shard_map/qhd,khd->hqk/dot_general | solution.py:49
  171.6 11.9 %fusion.1 = f32[12,512]{1,0:T(8,128)S(1)} fusion(f32[12,512]{1,0:T(8,128)S(1)} %get-tuple-element.85, f32[12,512,1024]{2,1,0:T(8,128)} %get-tuple-element.86, pred[512,1024]{1,0:T(8,128)(4,1)S(1)} %copy-done.9), kind=kLoop, calls=%fused_computation.13 | loop fusion | flops 25159680 | bytes 25739264 | tf_op jit(solution)/shard_map/reduce_sum | solution.py:115
  183.6 20.6 %multiply_reduce_fusion.1 = (f32[12,512]{1,0:T(8,128)S(1)}, f32[12,512,1024]{2,1,0:T(8,128)}) fusion(f32[12,512]{1,0:T(8,128)S(1)} %log_add_fusion.1, f32[12,512,1024]{2,1,0:T(8,128)} %get-tuple-element.88, pred[512,1024]{1,0:T(8,128)(4,1)S(1)} %copy-done.8, bf16[512,12,64]{0,2,1:T(8,128)(2,1)S(1)} %bitcast.82, f32[1024,3,12,64]{0,3,2,1:T(8,128)} %bitcast.76), kind=kOutput, calls=%fused_computation.4 | convolution fusion | flops 836757504 | bytes 53264384 | tf_op jit(solution)/shard_map/qhd,khd->hqk/dot_general | solution.py:181
  204.2 19.0 %multiply_reduce_fusion = (f32[12,512]{1,0:T(8,128)S(1)}, f32[12,512,1024]{2,1,0:T(8,128)}) fusion(f32[12,512]{1,0:T(8,128)S(1)} %log_add_fusion, f32[12,512,1024]{2,1,0:T(8,128)} %get-tuple-element.86, pred[512,1024]{1,0:T(8,128)(4,1)S(1)} %copy-done.9, bf16[512,12,64]{0,2,1:T(8,128)(2,1)} %bitcast.84, f32[1024,3,12,64]{0,3,2,1:T(8,128)} %bitcast.77), kind=kOutput, calls=%fused_computation.1 | convolution fusion | flops 836757504 | bytes 53264384 | tf_op jit(solution)/shard_map/qhd,khd->hqk/dot_general | solution.py:181
  223.2 42.4 %multiply_convert_fusion = (bf16[12,512,1024]{2,1,0:T(8,128)(2,1)}, bf16[12,512,1024]{2,1,0:T(8,128)(2,1)}) fusion(f32[12,512,1024]{2,1,0:T(8,128)} %get-tuple-element.92, f32[12,512]{1,0:T(8,128)S(1)} %get-tuple-element.91, f32[12,512]{1,0:T(8,128)S(1)} %log_add_fusion, f32[12,512,1024]{2,1,0:T(8,128)} %get-tuple-element.86, ...), kind=kLoop, calls=%fused_computation | loop fusion | flops 75497472 | bytes 126976000 | tf_op jit(solution)/shard_map/convert_element_type | solution.py:192
  265.7 8.6 multiply_bitcast_fusion.2
  274.3 10.2 %multiply_bitcast_fusion.1 = f32[512,12,64]{0,2,1:T(8,128)} fusion(bf16[12,512,1024]{2,1,0:T(8,128)(2,1)} %get-tuple-element.96, bf16[1024,12,48]{0,2,1:T(8,128)(2,1)} %copy-done.5, bf16[1024,12,8]{0,2,1:T(8,128)(2,1)S(1)} %copy-done.23, bf16[1024,12,8]{0,2,1:T(8,128)(2,1)S(1)} %copy-done.20), kind=kOutput, calls=%fused_computation.79 | convolution fusion | flops 810418176 | bytes 15728640 | tf_op jit(solution)/shard_map/hqk,khd->qhd/dot_general | solution.py:194
  284.4 3.1 fusion.20
  287.5 2.0 multiply_add_fusion.3
  289.5 2.3 fusion.32
  291.9 9.4 multiply_bitcast_fusion
  303.8 2.1 multiply_add_fusion.1
  305.9 9.2 fusion.27
  315.2 12.6 %fusion.26 = bf16[12,64,512]{2,1,0:T(8,128)(2,1)S(1)} fusion(f32[12,512]{1,0:T(8,128)S(1)} %copy-done.39, f32[12,512]{1,0:T(8,128)S(1)} %copy-done.37, f32[12,512,1024]{2,1,0:T(8,128)} %get-tuple-element.86, pred[512,1024]{1,0:T(8,128)(4,1)S(1)} %copy-done.10, f32[1024,3,12,64]{0,3,2,1:T(8,128)} %bitcast.79), kind=kOutput, calls=%fused_computation.81 | convolution fusion | flops 837156864 | bytes 28098560 | tf_op jit(solution)/shard_map/hqk,khd->qhd/dot_general | solution.py:119
  328.6 2.8 fusion.28
  331.5 2.3 add_bitcast_fusion.2
  335.0 12.1 %fusion.5 = f32[12,64,1024]{2,1,0:T(8,128)S(1)} fusion(bf16[512,12,64]{0,2,1:T(8,128)(2,1)S(1)} %bitcast.85, f32[12,512]{1,0:T(8,128)S(1)} %log_add_fusion, f32[12,512,1024]{2,1,0:T(8,128)} %get-tuple-element.86, pred[512,1024]{1,0:T(8,128)(4,1)S(1)} %copy-done.10), kind=kOutput, calls=%fused_computation.18 | convolution fusion | flops 830472192 | bytes 29646848 | tf_op jit(solution)/shard_map/hqk,qhd->khd/dot_general | solution.py:184
  347.2 11.9 %add_bitcast_fusion = bf16[1024,1,12,64]{0,3,2,1:T(8,128)(2,1)S(1)} fusion(f32[12,64,1024]{2,1,0:T(8,128)S(1)} %fusion.5, bf16[512,12,64]{0,2,1:T(8,128)(2,1)S(1)} %bitcast.83, f32[12,512]{1,0:T(8,128)S(1)} %copy-done.31, f32[12,512,1024]{2,1,0:T(8,128)} %get-tuple-element.88, pred[512,1024]{1,0:T(8,128)(4,1)S(1)} %copy-done.8), kind=kOutput, calls=%fused_computation.59 | convolution fusion | flops 832045056 | bytes 31219712 | tf_op jit(solution)/shard_map/hqk,qhd->khd/dot_general | solution.py:184
  359.9 2.1 copy-done.11
  362.0 6.5 fusion.49
  369.3 13.3 %all-gather = bf16[4,1,768]{2,1,0:T(2,128)(2,1)S(1)} all-gather(bf16[1,1,768]{2,1,0:T(2,128)(2,1)S(1)} %reshape.314), channel_id=1, replica_groups=mesh['rep'=8,'shard'=4] {'shard'}, dimensions={0}, use_global_device_ids=true | all-gather | bytes 7680 | tf_op jit(solution)/shard_map/all_gather | solution.py:85
  382.7 36.1 %multiply_convert_fusion.2 = (bf16[1024,3072]{1,0:T(8,128)(2,1)}, f32[1024,3072]{1,0:T(8,128)}, f32[1024,3072]{1,0:T(8,128)}) fusion(f32[3072]{0:T(1024)S(1)} %bitcast.87, bf16[768,3072]{1,0:T(8,128)(2,1)} %all-gather.10.cloned.1.call-done, f32[1024,768]{1,0:T(8,128)S(1)} %copy-done.1, f32[768]{0:T(1024)S(1)} %convert_element_type.100, ...), kind=kOutput, calls=%fused_computation.24 | convolution fusion | flops 5043388416 | bytes 39348224 | tf_op jit(solution)/shard_map/dot_general | solution.py:134
  418.7 18.2 %convert_reduce_fusion = (f32[3072]{0:T(1024)S(1)}, bf16[1024,3072]{1,0:T(8,128)(2,1)}) fusion(f32[1024,3072]{1,0:T(8,128)} %get-tuple-element.56, bf16[1024,768]{1,0:T(8,128)(2,1)} %get-tuple-element.68, bf16[3072,768]{1,0:T(8,128)(2,1)} %all-gather.12.cloned.1.call-done, f32[1024,3072]{1,0:T(8,128)} %get-tuple-element.84, f32[3072]{0:T(1024)S(1)} %bitcast.88), kind=kOutput, calls=%fused_computation.20 | convolution fusion | flops 4885312512 | bytes 37773312 | tf_op jit(solution)/shard_map/te,fe->tf/dot_general | solution.py:161
  436.9 10.6 %fusion.50 = f32[768,3072]{1,0:T(8,128)} fusion(bf16[1024,3072]{1,0:T(8,128)(2,1)} %get-tuple-element.95, f32[1024,768]{1,0:T(8,128)S(1)} %copy-done.1, f32[768]{0:T(1024)S(1)} %convert_element_type.100, f32[768]{0:T(1024)S(1)} %convert_element_type.99, f32[1024]{0:T(1024)S(1)} %copy-done.33, f32[1024]{0:T(1024)S(1)} %copy-done.29), kind=kOutput, calls=%fused_computation.130 | convolution fusion | flops 4835770368 | bytes 18888704 | tf_op jit(solution)/shard_map/td,tf->df/dot_general | solution.py:164
  447.6 10.1 %fusion.65 = f32[3072,768]{1,0:T(8,128)} fusion(bf16[1024,3072]{1,0:T(8,128)(2,1)} %get-tuple-element.55, bf16[1024,768]{1,0:T(8,128)(2,1)} %get-tuple-element.68), kind=kOutput, calls=%fused_computation.140 | convolution fusion | flops 4831838208 | bytes 17301504 | tf_op jit(solution)/shard_map/tf,te->fe/dot_general | solution.py:160
  459.9 6.8 fusion.64
  468.4 10.9 %multiply_reduce_fusion.2 = (f32[768]{0:T(1024)S(1)}, f32[1024]{0:T(1024)S(1)}, f32[1024]{0:T(1024)S(1)}, f32[768]{0:T(1024)S(1)}, f32[768]{0:T(1024)S(1)}, /*index=5*/f32[768]{0:T(1024)S(1)}, f32[1024,768]{1,0:T(8,128)}) fusion(f32[1024,768]{1,0:T(8,128)S(1)} %copy-done.1, f32[1024]{0:T(1024)S(1)} %copy-done.33, f32[1024]{0:T(1024)S(1)} %copy-done.29, ...), kind=kOutput, calls=%fused_computation.54 | convolution fusion | flops 4842842112 | bytes 20482048 | tf_op jit(solution)/shard_map/tf,df->td/dot_general | solution.py:165
  479.3 24.1 %reduce-scatter.5.cloned.1.call-done = f32[192,2304]{1,0:T(8,128)} async-done(((f32[768,2304]{1,0:T(8,128)}), f32[192,2304]{1,0:T(8,128)}) %reduce-scatter.5.cloned.1.call-update) | async-done | bytes 1769488 | tf_op jit(solution)/shard_map/reduce_scatter | solution.py:221
  503.4 164.2 %reduce-scatter.9.cloned.1.call-done = f32[192,3072]{1,0:T(8,128)} async-done(((f32[768,3072]{1,0:T(8,128)}), f32[192,3072]{1,0:T(8,128)}) %reduce-scatter.9.cloned.1.call-update) | async-done | bytes 2359312 | tf_op jit(solution)/shard_map/reduce_scatter | solution.py:225
  667.6 164.5 %reduce-scatter.11.cloned.1.call-done = f32[768,768]{1,0:T(8,128)} async-done(((f32[3072,768]{1,0:T(8,128)}), f32[768,768]{1,0:T(8,128)}) %reduce-scatter.11.cloned.1.call-update) | async-done | bytes 2359312 | tf_op jit(solution)/shard_map/reduce_scatter | solution.py:227
  832.8 19.0 %all-reduce.22 = (f32[768]{0:T(1024)S(1)}, f32[768]{0:T(1024)S(1)}, f32[768]{0:T(1024)S(1)}, f32[768]{0:T(1024)S(1)}, f32[2304]{0:T(1024)S(1)}, /*index=5*/f32[768]{0:T(1024)S(1)}, f32[3072]{0:T(1024)S(1)}) all-reduce(f32[768]{0:T(1024)S(1)} %get-tuple-element.19, ...), channel_id=2, replica_groups=mesh['rep'=8,'shard'=4] {'shard'}, use_global_device_ids=true, to_apply=%region_15.16.clone | all-reduce | flops 9216 | bytes 73728
  852.3 24.8 %all-reduce.20 = (f32[192]{0:T(256)}, f32[192]{0:T(256)}, f32[192]{0:T(256)}, f32[192]{0:T(256)}, f32[576]{0:T(1024)}, /*index=5*/f32[192]{0:T(256)S(1)}, f32[768]{0:T(1024)}) all-reduce(f32[192]{0:T(256)S(1)} %dynamic-slice.8, f32[192]{0:T(256)S(1)} %dynamic-slice.10, ...), channel_id=1, replica_groups=mesh['rep'=8,'shard'=4] {'rep'}, use_global_device_ids=true, to_apply=%region_16.17 | all-reduce | flops 2304 | bytes 18432 | tf_op jit(solution)/shard_map/psum | solution.py:230
  877.1 4.2 fusion.52
  881.3 2.2 add_add_fusion.2
  883.5 8.7 fusion.63
  892.3 3.2 add_add_fusion.3
  895.5 55.0 %all-reduce.26.cloned.1.call-done = (f32[192,2304]{1,0:T(8,128)}, f32[192,768]{1,0:T(8,128)}, f32[192,3072]{1,0:T(8,128)}, f32[768,768]{1,0:T(8,128)}) async-done(((f32[192,2304]{1,0:T(8,128)}, f32[192,768]{1,0:T(8,128)}, f32[192,3072]{1,0:T(8,128)}, f32[768,768]{1,0:T(8,128)}), (f32[192,2304]{1,0:T(8,128)}, f32[192,768]{1,0:T(8,128)}, f32[192,3072]{1,0:T(8,128)}, ...) | async-done | bytes 7077904 | tf_op jit(solution)/shard_map/psum | solution.py:230
  951.1 3.1 copy.47
  (242 shorter events, 23.3 us)
Async XLA Ops:
  7.3 29.2 %copy-start = (f32[1024,768]{1,0:T(8,128)S(1)}, f32[1024,768]{1,0:T(8,128)}, u32[]{:S(2)}) copy-start(f32[1024,768]{1,0:T(8,128)} %param.15) | copy-start | bytes 9437188
  7.3 38.3 %all-gather.8.cloned.1.call-start = ((), (), s32[]{:S(2)}) async-start(), calls=%async_computation.5 | async-start | bytes 1474560 | tf_op jit(solution)/shard_map/all_gather | solution.py:82
  8.0 106.5 %all-gather.6.cloned.1.call-start = ((), (), s32[]{:S(2)}) async-start(), calls=%async_computation.4 | async-start | bytes 4423680 | tf_op jit(solution)/shard_map/all_gather | solution.py:80
  8.8 373.9 %all-gather.10.cloned.1.call-start = ((), (), s32[]{:S(2)}) async-start(), calls=%async_computation.6 | async-start | bytes 5898240 | tf_op jit(solution)/shard_map/all_gather | solution.py:84
  9.5 28.3 %copy-start.40 = (s32[1024]{0:T(1024)S(1)}, s32[1024]{0:T(1024)}, u32[]{:S(2)}) copy-start(s32[1024]{0:T(1024)} %param.17) | copy-start | bytes 12292
  9.5 409.2 %all-gather.12.cloned.1.call-start = ((), (), s32[]{:S(2)}) async-start(), calls=%async_computation.7 | async-start | bytes 5898240 | tf_op jit(solution)/shard_map/all_gather | solution.py:86
  10.1 469.2 %reduce-scatter.7.cloned.1.call-start = ((), (), s32[]{:S(2)}) async-start(), calls=%async_computation.9 | async-start | bytes 2949120 | tf_op jit(solution)/shard_map/reduce_scatter | solution.py:223
  36.4 78.0 %copy-start.44 = (f32[768]{0:T(1024)}, f32[768]{0:T(1024)S(1)}, u32[]{:S(2)}) copy-start(f32[768]{0:T(1024)S(1)} %convert_element_type.90) | copy-start | bytes 9220
  36.4 78.0 %copy-start.46 = (f32[768]{0:T(1024)}, f32[768]{0:T(1024)S(1)}, u32[]{:S(2)}) copy-start(f32[768]{0:T(1024)S(1)} %convert_element_type.91) | copy-start | bytes 9220
  36.7 77.8 %copy-start.28 = (f32[1024]{0:T(1024)}, f32[1024]{0:T(1024)S(1)}, u32[]{:S(2)}) copy-start(f32[1024]{0:T(1024)S(1)} %broadcast_multiply_fusion) | copy-start | bytes 12292
  37.8 76.7 %copy-start.32 = (f32[1024]{0:T(1024)}, f32[1024]{0:T(1024)S(1)}, u32[]{:S(2)}) copy-start(f32[1024]{0:T(1024)S(1)} %fusion.38) | copy-start | bytes 12292
  136.6 129.0 %copy-start.5 = (bf16[1024,12,48]{0,2,1:T(8,128)(2,1)}, bf16[1024,12,48]{0,2,1:T(8,128)(2,1)S(1)}, u32[]{:S(2)}) copy-start(bf16[1024,12,48]{0,2,1:T(8,128)(2,1)S(1)} %slice.136) | copy-start | bytes 3538948
  136.8 23.5 %copy-start.18 = (bf16[1024,12,8]{0,2,1:T(8,128)(2,1)}, bf16[1024,12,8]{0,2,1:T(8,128)(2,1)S(1)}, u32[]{:S(2)}) copy-start(bf16[1024,12,8]{0,2,1:T(8,128)(2,1)S(1)} %get-tuple-element.61) | copy-start | bytes 589828
  136.8 23.5 %copy-start.21 = (bf16[1024,12,8]{0,2,1:T(8,128)(2,1)}, bf16[1024,12,8]{0,2,1:T(8,128)(2,1)S(1)}, u32[]{:S(2)}) copy-start(bf16[1024,12,8]{0,2,1:T(8,128)(2,1)S(1)} %get-tuple-element.62) | copy-start | bytes 589828
  137.0 23.4 %copy-start.6 = (bf16[1024,12,64]{0,2,1:T(8,128)(2,1)}, bf16[1024,12,64]{0,2,1:T(8,128)(2,1)S(1)}, u32[]{:S(2)}) copy-start(bf16[1024,12,64]{0,2,1:T(8,128)(2,1)S(1)} %pad_maximum_fusion) | copy-start | bytes 4718596
  148.4 11.9 %copy-start.34 = (f32[12,512]{1,0:T(8,128)}, f32[12,512]{1,0:T(8,128)S(1)}, u32[]{:S(2)}) copy-start(f32[12,512]{1,0:T(8,128)S(1)} %get-tuple-element.87) | copy-start | bytes 73732
  148.4 12.0 %copy-start.9 = (pred[512,1024]{1,0:T(8,128)(4,1)S(1)}, pred[512,1024]{1,0:T(8,128)(4,1)}, u32[]{:S(2)}) copy-start(pred[512,1024]{1,0:T(8,128)(4,1)} %get-tuple-element.79) | copy-start | bytes 1572868
  160.3 11.3 %copy-start.35 = (f32[12,512]{1,0:T(8,128)}, f32[12,512]{1,0:T(8,128)S(1)}, u32[]{:S(2)}) copy-start(f32[12,512]{1,0:T(8,128)S(1)} %fusion) | copy-start | bytes 73732
  160.3 62.9 %copy-start.30 = (f32[12,512]{1,0:T(8,128)}, f32[12,512]{1,0:T(8,128)S(1)}, u32[]{:S(2)}) copy-start(f32[12,512]{1,0:T(8,128)S(1)} %log_add_fusion.1) | copy-start | bytes 73732
  171.6 11.9 %copy-start.36 = (f32[12,512]{1,0:T(8,128)}, f32[12,512]{1,0:T(8,128)S(1)}, u32[]{:S(2)}) copy-start(f32[12,512]{1,0:T(8,128)S(1)} %get-tuple-element.85) | copy-start | bytes 73732
  171.6 12.0 %copy-start.13 = (bf16[512,768]{0,1:T(8,128)(2,1)S(1)}, bf16[512,768]{0,1:T(8,128)(2,1)}, u32[]{:S(2)}) copy-start(bf16[512,768]{0,1:T(8,128)(2,1)} %get-tuple-element.69) | copy-start | bytes 2359300
  183.5 20.7 %copy-start.38 = (f32[12,512]{1,0:T(8,128)}, f32[12,512]{1,0:T(8,128)S(1)}, u32[]{:S(2)}) copy-start(f32[12,512]{1,0:T(8,128)S(1)} %fusion.1) | copy-start | bytes 73732
  223.2 42.4 %copy-start.19 = (bf16[1024,12,8]{0,2,1:T(8,128)(2,1)S(1)}, bf16[1024,12,8]{0,2,1:T(8,128)(2,1)}, u32[]{:S(2)}) copy-start(bf16[1024,12,8]{0,2,1:T(8,128)(2,1)} %copy-done.18) | copy-start | bytes 589828
  223.2 42.4 %copy-start.22 = (bf16[1024,12,8]{0,2,1:T(8,128)(2,1)S(1)}, bf16[1024,12,8]{0,2,1:T(8,128)(2,1)}, u32[]{:S(2)}) copy-start(bf16[1024,12,8]{0,2,1:T(8,128)(2,1)} %copy-done.21) | copy-start | bytes 589828
  265.6 8.6 copy-start.20
  274.3 15.2 %slice-start.6 = ((s8[12582912]{0:T(1024)(128)(4,1)}), s8[4194304]{0:T(1024)(128)(4,1)S(1)}, s32[]{:S(2)}) async-start(s8[12582912]{0:T(1024)(128)(4,1)} %bitcast.73), calls=%async_computation.19 | async-start | bytes 8388608
  274.3 15.2 %slice-start.7 = ((s8[12582912]{0:T(1024)(128)(4,1)}), s8[4194304]{0:T(1024)(128)(4,1)S(1)}, s32[]{:S(2)}) async-start(s8[12582912]{0:T(1024)(128)(4,1)} %bitcast.73), calls=%async_computation.20 | async-start | bytes 8388608
  289.5 16.4 %slice-start = ((s8[25165824]{0:T(1024)(128)(4,1)}), s8[4194304]{0:T(1024)(128)(4,1)S(1)}, s32[]{:S(2)}) async-start(s8[25165824]{0:T(1024)(128)(4,1)} %bitcast.71), calls=%async_computation.13 | async-start | bytes 8388608
  289.5 16.4 %slice-start.1 = ((s8[25165824]{0:T(1024)(128)(4,1)}), s8[4194304]{0:T(1024)(128)(4,1)S(1)}, s32[]{:S(2)}) async-start(s8[25165824]{0:T(1024)(128)(4,1)} %bitcast.71), calls=%async_computation.14 | async-start | bytes 8388608
  289.5 16.3 %slice-start.2 = ((s8[25165824]{0:T(1024)(128)(4,1)}), s8[4194304]{0:T(1024)(128)(4,1)S(1)}, s32[]{:S(2)}) async-start(s8[25165824]{0:T(1024)(128)(4,1)} %bitcast.71), calls=%async_computation.15 | async-start | bytes 8388608
  291.9 14.0 %slice-start.3 = ((s8[25165824]{0:T(1024)(128)(4,1)}), s8[4194304]{0:T(1024)(128)(4,1)S(1)}, s32[]{:S(2)}) async-start(s8[25165824]{0:T(1024)(128)(4,1)} %bitcast.71), calls=%async_computation.16 | async-start | bytes 8388608
  291.9 14.0 %slice-start.4 = ((s8[25165824]{0:T(1024)(128)(4,1)}), s8[4194304]{0:T(1024)(128)(4,1)S(1)}, s32[]{:S(2)}) async-start(s8[25165824]{0:T(1024)(128)(4,1)} %bitcast.71), calls=%async_computation.17 | async-start | bytes 8388608
  291.9 14.0 %slice-start.5 = ((s8[25165824]{0:T(1024)(128)(4,1)}), s8[4194304]{0:T(1024)(128)(4,1)S(1)}, s32[]{:S(2)}) async-start(s8[25165824]{0:T(1024)(128)(4,1)} %bitcast.71), calls=%async_computation.18 | async-start | bytes 8388608
  305.9 9.2 copy-start.10
  305.9 9.2 copy-start.37
  305.9 9.2 copy-start.39
  315.1 12.6 %copy-start.63 = (bf16[12,64,512]{2,1,0:T(8,128)(2,1)}, bf16[12,64,512]{2,1,0:T(8,128)(2,1)S(1)}, u32[]{:S(2)}) copy-start(bf16[12,64,512]{2,1,0:T(8,128)(2,1)S(1)} %fusion.27) | copy-start | bytes 2359300
  315.1 13.5 %copy-start.24 = (bf16[1024,768]{1,0:T(8,128)(2,1)S(1)}, bf16[1024,768]{1,0:T(8,128)(2,1)}, u32[]{:S(2)}) copy-start(bf16[1024,768]{1,0:T(8,128)(2,1)} %get-tuple-element.68) | copy-start | bytes 4718596
  331.4 172.0 %reduce-scatter.5.cloned.1.call-start = ((), (), s32[]{:S(2)}) async-start(), calls=%async_computation.8 | async-start | bytes 8847360 | tf_op jit(solution)/shard_map/reduce_scatter | solution.py:221
  335.0 12.1 %copy-start.14 = (bf16[512,768]{0,1:T(8,128)(2,1)S(1)}, bf16[512,768]{0,1:T(8,128)(2,1)}, u32[]{:S(2)}) copy-start(bf16[512,768]{0,1:T(8,128)(2,1)} %get-tuple-element.69) | copy-start | bytes 2359300
  335.0 12.1 %copy-start.31 = (f32[12,512]{1,0:T(8,128)S(1)}, f32[12,512]{1,0:T(8,128)}, u32[]{:S(2)}) copy-start(f32[12,512]{1,0:T(8,128)} %copy-done.30) | copy-start | bytes 73732
  368.6 299.0 %reduce-scatter.9.cloned.1.call-start = ((), (), s32[]{:S(2)}) async-start(), calls=%async_computation.10 | async-start | bytes 11796480 | tf_op jit(solution)/shard_map/reduce_scatter | solution.py:225
  447.6 384.5 %reduce-scatter.11.cloned.1.call-start = ((), (), s32[]{:S(2)}) async-start(), calls=%async_computation.11 | async-start | bytes 11796480 | tf_op jit(solution)/shard_map/reduce_scatter | solution.py:227
  457.8 492.8 %all-reduce.26.cloned.1.call-start = ((), (), s32[]{:S(2)}) async-start(), calls=%async_computation.12 | async-start | bytes 14155776 | tf_op jit(solution)/shard_map/psum | solution.py:230
  877.1 73.5 %copy-start.55 = (f32[192]{0:T(256)}, f32[192]{0:T(256)S(1)}, u32[]{:S(2)}) copy-start(f32[192]{0:T(256)S(1)} %get-tuple-element.135) | copy-start | bytes 2308
  883.5 8.7 copy-start.56
  883.5 8.8 copy-start.64
  883.5 8.8 copy-start.66
  (38 other events, 117.0 us)
Sparse Core Ops, SparseCore 0:
  9.7 33.8 all-gather.7
  45.2 69.2 all-gather.5
  116.0 87.9 all-gather.9
  205.5 87.8 all-gather.11
  331.5 46.6 reduce-scatter.6
  380.4 123.0 reduce-scatter.4
  505.8 161.7 reduce-scatter.8
  669.9 162.1 reduce-scatter.10
  835.8 114.7 all-reduce.25
where the time goes:
time: 968 us; the launch traced here: 965 us
  waiting for transfers between devices  475 us (49%)
  matrix products  264 us (27%)
  other arithmetic  91.6 us (9%)
  blocking collectives  79.7 us (8%)
  local copies, waits for them, and re-layouts  35.7 us (4%)
  between operations  18.4 us (2%)
    reduce_scatter x1, waiting for transfers between devices, body(): lax.psum_scatter(down_weight_g, 'shard', scatter_dimension=0, tiled=True)  165 us
    reduce_scatter x1, waiting for transfers between devices, body(): lax.psum_scatter(up_weight_g, 'shard', scatter_dimension=0, tiled=True)  164 us
    all_gather x1, waiting for transfers between devices, body(): lax.all_gather(qkv_weight, 'shard', axis=0, tiled=True)  64.5 us
    psum x1, waiting for transfers between devices, body(): lax.psum((all_owned[0], all_owned[1], all_owned[2], all_owned[3], all_own...  55 us
    convert_element_type x1, other arithmetic, body(): scores_grad = (probs * (probs_grad - jnp.sum(probs_grad * probs, axis=-1,...  42.4 us
    unnamed x2, blocking collectives  41.6 us
    dot_general x2, matrix products, body(): jnp.einsum('qhd,khd->hqk', grad_block, value_b, preferred_element_type=jn...  39.6 us
    dot_general x1, matrix products, body(): jnp.dot(second_b, gathered[8], preferred_element_type=jnp.float32)  36.1 us
  transfers between devices with their start and end apart: 9, of which 5 were waited for; matrix products, arithmetic and copies ran while one was open for 39% of the time, Pallas kernels for 0%

commit v1 on v0

--- a/solution.py
+++ b/solution.py
@@ -1,6 +1,10 @@
+import functools
+
 import jax
 import jax.numpy as jnp
 from jax import lax
+from jax.experimental import pallas as pl
+from jax.experimental.pallas import tpu as pltpu
 from jax.sharding import PartitionSpec as P
 
 D = 768
@@ -20,9 +24,8 @@
 
 def seq_positions(segments):
     row_index = jnp.arange(segments.shape[0], dtype=jnp.int32)
-    previous = jnp.concatenate([jnp.full((1,), -1, jnp.int32), segments[:-1]])
-    starts = jnp.where(segments != previous, row_index, 0)
-    return row_index - lax.cummax(starts, axis=0)
+    before = jnp.sum((segments[:, None] > segments[None, :]).astype(jnp.int32), axis=1)
+    return row_index - before
 
 
 def rotate(heads_in, places):
@@ -53,6 +56,169 @@
     seg_here = segments[first_row : first_row + block_rows]
     allowed = (seg_here[:, None] == segments[None, :]) & (row_index[None, :] <= rows_here[:, None])
     return (jnp.where(allowed[None], raw_scores, -1e30), q_block)
+
+
+def plane_bits(rep_size):
+    bits, b = [], 1
+    while b < rep_size:
+        bits.append(b)
+        b *= 2
+    return bits
+
+
+def swap(value, axis, bit):
+    size = lax.axis_size(axis)
+    return lax.ppermute(value, axis, [(i, i ^ bit) for i in range(size)])
+
+
+def place_ids():
+    rep = lax.axis_index("rep")
+    return lax.axis_index("shard"), (rep // 2) % 4, rep % 2
+
+
+def gather_start(shard):
+    rows, cols = shard.shape
+    z, q, c = place_ids()
+    piece = lax.dynamic_slice(shard, (q * (rows // 4), c * (cols // 2)), (rows // 4, cols // 2))
+    far = jnp.stack([swap(piece, "shard", k) for k in (1, 2, 3)])
+    parts = [far] + [swap(far, "rep", j * 2) for j in (1, 2, 3)]
+    other = [swap(p, "rep", 1) for p in parts]
+    return parts + other
+
+
+def assemble_body(rows, cols, ids_ref, shard_ref, *refs):
+    pieces, out_ref, sem = refs[:8], refs[8], refs[9]
+    z, q, c = ids_ref[0], ids_ref[1], ids_ref[2]
+    part = rows // 4
+    half = cols // 2
+    copies = [
+        pltpu.make_async_copy(
+            shard_ref, out_ref.at[pl.ds(pl.multiple_of(z * rows, rows), rows)], sem
+        )
+    ]
+    for index in range(8):
+        j, h = index % 4, index // 4
+        col = pl.multiple_of((c ^ h) * half, half)
+        for k in (1, 2, 3):
+            row = pl.multiple_of((z ^ k) * rows + (q ^ j) * part, part)
+            copies.append(
+                pltpu.make_async_copy(
+                    pieces[index].at[k - 1],
+                    out_ref.at[pl.ds(row, part), pl.ds(col, half)],
+                    sem,
+                )
+            )
+    for copy in copies:
+        copy.start()
+    for copy in copies:
+        copy.wait()
+
+
+def assemble(ids, shard, pieces):
+    rows, cols = shard.shape
+    anywhere = pl.BlockSpec(memory_space=pl.ANY)
+    return pl.pallas_call(
+        functools.partial(assemble_body, rows, cols),
+        out_shape=jax.ShapeDtypeStruct((4 * rows, cols), shard.dtype),
+        in_specs=[pl.BlockSpec(memory_space=pltpu.SMEM)] + [anywhere] * 9,
+        out_specs=anywhere,
+        scratch_shapes=[pltpu.SemaphoreType.DMA],
+        name="assemble",
+    )(ids, shard, *pieces)
+
+
+def pair(left, right):
+    return left.astype(jnp.float32) + right.astype(jnp.float32)
+
+
+def reduce_rows(grad):
+    total_rows, cols = grad.shape
+    rows = total_rows // 4
+    z, q, c = place_ids()
+    y_bit, x_bit = q // 2, q % 2
+    half = cols // 2
+    send = lax.dynamic_slice(grad, (0, (1 - c) * half), (total_rows, half))
+    keep = lax.dynamic_slice(grad, (0, c * half), (total_rows, half))
+    got = swap(send, "rep", 1)
+    one = pair(keep, got).astype(jnp.bfloat16).reshape(4, 2, 2, rows // 4, half)
+
+    def halves(block, bit, axis):
+        mine = lax.dynamic_index_in_dim(block, bit, axis, keepdims=False)
+        theirs = lax.dynamic_index_in_dim(block, 1 - bit, axis, keepdims=False)
+        return mine, theirs
+
+    low, high = one[:2], one[2:]
+    low_mine, low_theirs = halves(low, x_bit, 2)
+    high_mine, high_theirs = halves(high, y_bit, 1)
+    low = pair(low_mine, swap(low_theirs, "rep", 2)).astype(jnp.bfloat16)
+    high = pair(high_mine, swap(high_theirs, "rep", 4)).astype(jnp.bfloat16)
+    low_mine, low_theirs = halves(low, y_bit, 1)
+    high_mine, high_theirs = halves(high, x_bit, 1)
+    low_got = swap(low_theirs, "rep", 4)
+    high_got = swap(high_theirs, "rep", 2)
+    two = jnp.concatenate([pair(low_mine, low_got), pair(high_mine, high_got)]).astype(
+        jnp.bfloat16
+    )
+    pieces = [lax.dynamic_index_in_dim(two, z ^ k, 0, keepdims=False) for k in range(4)]
+    got = [swap(pieces[k], "shard", k) for k in (1, 2, 3)]
+    three = (pair(pieces[0], got[0]) + pair(got[1], got[2])).astype(jnp.bfloat16)
+    for bit in plane_bits(lax.axis_size("rep"))[3:]:
+        three = pair(three, swap(three, "rep", bit)).astype(jnp.bfloat16)
+    parts = [three] + [swap(three, "rep", j * 2) for j in (1, 2, 3)]
+    other = [swap(p, "rep", 1) for p in parts]
+    return parts + other
+
+
+def place_body(part, half, ids_ref, *refs):
+    pieces, out_ref = refs[:8], refs[8]
+    q, c = ids_ref[1], ids_ref[2]
+    for index in range(8):
+        j, h = index % 4, index // 4
+        row = pl.multiple_of((q ^ j) * part, part)
+        col = pl.multiple_of((c ^ h) * half, half)
+        out_ref[pl.ds(row, part), pl.ds(col, half)] = pieces[index][...].astype(jnp.float32)
+
+
+def place(ids, pieces):
+    part, half = pieces[0].shape
+    vmem = pl.BlockSpec(memory_space=pltpu.VMEM)
+    return pl.pallas_call(
+        functools.partial(place_body, part, half),
+        out_shape=jax.ShapeDtypeStruct((4 * part, 2 * half), jnp.float32),
+        in_specs=[pl.BlockSpec(memory_space=pltpu.SMEM)] + [vmem] * 8,
+        out_specs=vmem,
+        compiler_params=pltpu.CompilerParams(vmem_limit_bytes=32 * 2**20),
+        name="place",
+    )(ids, *pieces)
+
+
+def sum_small(vector):
+    for bit in plane_bits(lax.axis_size("rep")):
+        if bit in (2, 4):
+            continue
+        vector = vector + swap(vector, "rep", bit)
+    vector = (vector + swap(vector, "rep", 2)) + (swap(vector, "rep", 4) + swap(vector, "rep", 6))
+    return (vector + swap(vector, "shard", 1)) + (swap(vector, "shard", 2) + swap(vector, "shard", 3))
+
+
+def pack(vectors):
+    flat = jnp.concatenate([v.reshape(-1) for v in vectors])
+    fill = -flat.shape[0] % 1024
+    return jnp.concatenate([flat, jnp.zeros((fill,), flat.dtype)]).reshape(-1, 128)
+
+
+def gather_small(vectors):
+    packed = pack(vectors)
+    z = lax.axis_index("shard")
+    near = jnp.stack([packed] + [swap(packed, "shard", k) for k in (1, 2, 3)])
+    rows = jnp.stack(
+        [lax.dynamic_index_in_dim(near, z ^ i, 0, keepdims=False) for i in range(4)]
+    ).reshape(4, -1)
+    out, at = [], 0
+    for v in vectors:
+        out.append(rows[:, at : at + v.shape[0]].reshape(-1).astype(jnp.float32))
+        at += v.shape[0]
+    return out
 
 
 def body(
@@ -72,19 +238,27 @@
     down_weight,
     down_bias,
 ):
+    ids = jnp.stack(place_ids()).astype(jnp.int32)
+    small = gather_small(
+        [first_gain, first_shift, second_gain, second_shift, qkv_bias, out_bias, up_bias, down_bias]
+    )
+    qkv_full = assemble(ids, qkv_weight, gather_start(qkv_weight))
+    out_full = assemble(ids, out_weight, gather_start(out_weight))
+    up_full = assemble(ids, up_weight, gather_start(up_weight))
+    down_full = assemble(ids, down_weight, gather_start(down_weight))
     gathered = (
-        lax.all_gather(first_gain, "shard", axis=0, tiled=True),
-        lax.all_gather(first_shift, "shard", axis=0, tiled=True),
-        lax.all_gather(second_gain, "shard", axis=0, tiled=True),
-        lax.all_gather(second_shift, "shard", axis=0, tiled=True),
-        lax.all_gather(qkv_weight, "shard", axis=0, tiled=True),
-        lax.all_gather(qkv_bias, "shard", axis=0, tiled=True),
-        lax.all_gather(out_weight, "shard", axis=0, tiled=True),
-        lax.all_gather(out_bias, "shard", axis=0, tiled=True),
-        lax.all_gather(up_weight, "shard", axis=0, tiled=True),
-        lax.all_gather(up_bias, "shard", axis=0, tiled=True),
-        lax.all_gather(down_weight, "shard", axis=0, tiled=True),
-        lax.all_gather(down_bias, "shard", axis=0, tiled=True),
+        small[0],
+        small[1],
+        small[2],
+        small[3],
+        qkv_full,
+        small[4],
+        out_full,
+        small[5],
+        up_full,
+        small[6],
+        down_full,
+        small[7],
     )
     tokens_here = hidden_in.shape[0]
     score_scale = HD ** (-0.5)
@@ -140,20 +314,7 @@
         11
     ].astype(jnp.float32)
     output = hidden_in + attn_out + mlp_out
-    back_weights = (
-        lax.all_gather(first_gain, "shard", axis=0, tiled=True),
-        lax.all_gather(first_shift, "shard", axis=0, tiled=True),
-        lax.all_gather(second_gain, "shard", axis=0, tiled=True),
-        lax.all_gather(second_shift, "shard", axis=0, tiled=True),
-        lax.all_gather(qkv_weight, "shard", axis=0, tiled=True),
-        lax.all_gather(qkv_bias, "shard", axis=0, tiled=True),
-        lax.all_gather(out_weight, "shard", axis=0, tiled=True),
-        lax.all_gather(out_bias, "shard", axis=0, tiled=True),
-        lax.all_gather(up_weight, "shard", axis=0, tiled=True),
-        lax.all_gather(up_bias, "shard", axis=0, tiled=True),
-        lax.all_gather(down_weight, "shard", axis=0, tiled=True),
-        lax.all_gather(down_bias, "shard", axis=0, tiled=True),
-    )
+    back_weights = gathered
     cot_b = cotangent.astype(jnp.bfloat16)
     bias_out_g = jnp.sum(cotangent, axis=0)
     out_weight_g = jnp.einsum("td,te->de", mixed_b, cot_b, preferred_element_type=jnp.float32)
@@ -213,37 +374,28 @@
     )
     first_x_grad, first_gain_g, first_shift_g = pull_first(first_in_grad)
     input_grad = cotangent + first_x_grad + second_x_grad
-    all_owned = (
-        lax.psum_scatter(first_gain_g, "shard", scatter_dimension=0, tiled=True),
-        lax.psum_scatter(first_shift_g, "shard", scatter_dimension=0, tiled=True),
-        lax.psum_scatter(second_gain_g, "shard", scatter_dimension=0, tiled=True),
-        lax.psum_scatter(second_shift_g, "shard", scatter_dimension=0, tiled=True),
-        lax.psum_scatter(qkv_weight_g, "shard", scatter_dimension=0, tiled=True),
-        lax.psum_scatter(qkv_bias_g, "shard", scatter_dimension=0, tiled=True),
-        lax.psum_scatter(out_weight_g, "shard", scatter_dimension=0, tiled=True),
-        lax.psum_scatter(bias_out_g, "shard", scatter_dimension=0, tiled=True),
-        lax.psum_scatter(up_weight_g, "shard", scatter_dimension=0, tiled=True),
-        lax.psum_scatter(up_bias_g, "shard", scatter_dimension=0, tiled=True),
-        lax.psum_scatter(down_weight_g, "shard", scatter_dimension=0, tiled=True),
-        lax.psum_scatter(bias_out_g, "shard", scatter_dimension=0, tiled=True),
-    )
-    summed = lax.psum(
-        (
-            all_owned[0],
-            all_owned[1],
-            all_owned[2],
-            all_owned[3],
-            all_owned[4],
-            all_owned[5],
-            all_owned[6],
-            all_owned[7],
-            all_owned[8],
-            all_owned[9],
-            all_owned[10],
-            all_owned[11],
-        ),
-        "rep",
-    )
+    small_sum = sum_small(
+        pack(
+            [
+                first_gain_g,
+                first_shift_g,
+                second_gain_g,
+                second_shift_g,
+                qkv_bias_g,
+                bias_out_g,
+                up_bias_g,
+            ]
+        )
+    ).reshape(-1)
+    z = lax.axis_index("shard")
+    summed, at = [], 0
+    for size in (D, D, D, D, 3 * D, D, up_bias_g.shape[0]):
+        summed.append(lax.dynamic_slice(small_sum, (at + z * (size // 4),), (size // 4,)))
+        at += size
+    weight_sums = [
+        place(ids, reduce_rows(g.astype(jnp.bfloat16)))
+        for g in (qkv_weight_g, out_weight_g, up_weight_g, down_weight_g)
+    ]
     return (
         output,
         input_grad,
@@ -251,14 +403,14 @@
         summed[1],
         summed[2],
         summed[3],
+        weight_sums[0],
         summed[4],
+        weight_sums[1],
         summed[5],
+        weight_sums[2],
         summed[6],
-        summed[7],
-        summed[8],
-        summed[9],
-        summed[10],
-        summed[11],
+        weight_sums[3],
+        summed[5],
     )
 
 

time: 968 us -> 1100 us (1.14)
  Pallas kernels: 0 us -> 443 us
  waiting for transfers between devices: 475 us -> 114 us
  starting transfers between devices: 0.36 us -> 108 us
  blocking collectives: 79.7 us -> 0 us
  local copies, waits for them, and re-layouts: 35.7 us -> 64.2 us
  between operations: 18.4 us -> 2.32 us
    pallas_call x0 -> x8, Pallas kernels: none -> 443 us  [the longest x4 436 us: assemble(): pl.pallas_call(functools.partial(assemble_body, rows, cols), out_shape=ja...]
    reduce_scatter x4 -> x0, waiting for transfers between devices: 353 us -> none  [the longest x1 165 us: body(): lax.psum_scatter(down_weight_g, 'shard', scatter_dimension=0, tiled=True)]
    ppermute x0 -> x110, waiting for transfers between devices: none -> 114 us  [swap(): return lax.ppermute(value, axis, [(i, i ^ bit) for i in range(size)])]
    ppermute x0 -> x110, starting transfers between devices: none -> 108 us  [swap(): return lax.ppermute(value, axis, [(i, i ^ bit) for i in range(size)])]
    all_gather x4 -> x0, waiting for transfers between devices: 64.5 us -> none  [the longest x1 64.5 us: body(): lax.all_gather(qkv_weight, 'shard', axis=0, tiled=True)]
    psum x1 -> x0, waiting for transfers between devices: 55 us -> none  [body(): lax.psum((all_owned[0], all_owned[1], all_owned[2], all_owned[3], all_own...]
    unnamed x2 -> x0, blocking collectives: 41.6 us -> none
    psum x1 -> x0, blocking collectives: 24.8 us -> none  [body(): lax.psum((all_owned[0], all_owned[1], all_owned[2], all_owned[3], all_own...]
  transfers between devices with their start and end apart: 9 -> 110, of which waited for: 5 -> 33; matrix products, arithmetic and copies ran while one was open for 39% -> 37% of each run, Pallas kernels for 0% -> 40%
where the time goes in v1:
time: 1100 us; the launch traced here: 1090 us
  Pallas kernels  443 us (40%)
  matrix products  261 us (24%)
  waiting for transfers between devices  114 us (10%)
  starting transfers between devices  108 us (10%)
  other arithmetic  98.1 us (9%)
  local copies, waits for them, and re-layouts  64.2 us (6%)
    pallas_call x4, Pallas kernels, assemble(): pl.pallas_call(functools.partial(assemble_body, rows, cols), out_shape=ja...  436 us
    ppermute x110, waiting for transfers between devices, swap(): return lax.ppermute(value, axis, [(i, i ^ bit) for i in range(size)])  114 us
    ppermute x110, starting transfers between devices, swap(): return lax.ppermute(value, axis, [(i, i ^ bit) for i in range(size)])  108 us
    convert_element_type x1, other arithmetic, body(): scores_grad = (probs * (probs_grad - jnp.sum(probs_grad * probs, axis=-1,...  41.9 us
    dot_general x2, matrix products, body(): jnp.einsum('qhd,khd->hqk', grad_block, value_b, preferred_element_type=jn...  39.9 us
    dot_general x1, matrix products, body(): jnp.dot(second_b, gathered[8], preferred_element_type=jnp.float32)  37.5 us
    dot_general x2, matrix products, body(): jnp.einsum('hqk,qhd->khd', probs.astype(jnp.bfloat16), grad_block, prefer...  28.5 us
    reduce_sum x2, other arithmetic, body(): total = jnp.sum(expo_scores, axis=-1, keepdims=True)  24.9 us
  transfers between devices with their start and end apart: 110, of which 33 were waited for; matrix products, arithmetic and copies ran while one was open for 37% of the time, Pallas kernels for 40%

profile of v1, /device:TPU:0, one launch (start us, length us, event | category | flops | bytes accessed | tf_op | source)
XLA Modules:
  0.0 1091.9 jit_solution(7232142322587125407)
XLA Ops:
  0.7 5.7 concatenate.42
  6.4 5.1 collective-permute-start.2
  12.9 3.7 collective-permute-start.15
  32.9 3.7 collective-permute-start.5
  65.0 10.9 %collective-permute-start.33 = (bf16[192,384]{1,0:T(8,128)(2,1)}, bf16[192,384]{1,0:T(8,128)(2,1)S(1)}, u32[]{:S(2)}, u32[]{:S(2)}) collective-permute-start(bf16[192,384]{1,0:T(8,128)(2,1)} %dynamic_slice.237), channel_id=1, source_target_pairs={{0,1},{1,0},{2,3},{3,2},{4,5},{5,4},{6,7},{7,6},{8,9},{9,8},{10,11... | collective-permute-start | bytes 442376 | tf_op jit(solution)/shard_map/ppermute | solution.py:71
  87.8 37.5 %assemble.5 = bf16[768,768]{1,0:T(8,128)(2,1)} custom-call(s32[3]{0:T(128)} %pad_add_fusion.ids_ref, bf16[192,768]{1,0:T(8,128)(2,1)} %shard_ref.5, bf16[3,48,384]{2,1,0:T(8,128)(2,1)} %copy-done.38, bf16[3,48,384]{2,1,0:T(8,128)(2,1)} %collective-permute-done.16.refs_1_, bf16[3,48,384]{2,1,0:T(8,128)(2,1)} %collective-permute-done.17.refs_2_, ...), custom_call_target="tpu_custom_call" | custom-call | tf_op jit(solution)/shard_map/assemble/pallas_call | solution.py:120
  136.0 109.0 %assemble.4 = bf16[768,2304]{1,0:T(8,128)(2,1)} custom-call(s32[3]{0:T(128)} %pad_add_fusion.ids_ref, bf16[192,2304]{1,0:T(8,128)(2,1)} %shard_ref.4, bf16[3,48,1152]{2,1,0:T(8,128)(2,1)} %copy-done.30, bf16[3,48,1152]{2,1,0:T(8,128)(2,1)} %collective-permute-done.6.refs_1_, bf16[3,48,1152]{2,1,0:T(8,128)(2,1)} %collective-permute-done.7.refs_2_, ...), custom_call_target="tpu_custom_call" | custom-call | tf_op jit(solution)/shard_map/assemble/pallas_call | solution.py:120
  245.1 8.6 convolution_add_fusion
  253.6 9.6 copy.49
  268.0 10.8 fusion.26
  278.9 12.6 %fusion.1 = f32[12,512]{1,0:T(8,128)S(1)} fusion(f32[12,512]{1,0:T(8,128)S(1)} %get-tuple-element.108, f32[12,512,1024]{2,1,0:T(8,128)} %get-tuple-element.109, pred[512,1024]{1,0:T(8,128)(4,1)S(1)} %copy-done.16), kind=kLoop, calls=%fused_computation.13 | loop fusion | flops 25159680 | bytes 25739264 | tf_op jit(solution)/shard_map/reduce_sum | solution.py:289
  294.2 9.4 fusion.34
  303.7 13.4 %fusion.5 = f32[12,64,1024]{2,1,0:T(8,128)} fusion(bf16[512,12,64]{0,2,1:T(8,128)(2,1)} %bitcast.289, f32[12,512]{1,0:T(8,128)S(1)} %log_add_fusion, f32[12,512,1024]{2,1,0:T(8,128)} %get-tuple-element.109, pred[512,1024]{1,0:T(8,128)(4,1)S(1)} %copy-done.16), kind=kOutput, calls=%fused_computation.18 | convolution fusion | flops 830472192 | bytes 29646848 | tf_op jit(solution)/shard_map/hqk,qhd->khd/dot_general | solution.py:345
  317.1 21.3 %multiply_reduce_fusion = (f32[12,512]{1,0:T(8,128)}, f32[12,512,1024]{2,1,0:T(8,128)}) fusion(f32[12,512]{1,0:T(8,128)S(1)} %log_add_fusion, f32[12,512,1024]{2,1,0:T(8,128)} %get-tuple-element.109, pred[512,1024]{1,0:T(8,128)(4,1)S(1)} %copy-done.17, bf16[512,12,64]{0,2,1:T(8,128)(2,1)S(1)} %bitcast.290, f32[1024,3,12,64]{0,3,2,1:T(8,128)} %bitcast.272), kind=kOutput, calls=%fused_computation.1 | convolution fusion | flops 836757504 | bytes 53264384 | tf_op jit(solution)/shard_map/qhd,khd->hqk/dot_general | solution.py:342
  338.4 12.4 %fusion.25 = (f32[12,512]{1,0:T(8,128)S(1)}, f32[12,512,1024]{2,1,0:T(8,128)}) fusion(pred[512,1024]{1,0:T(8,128)(4,1)S(1)} %copy-done.15, bf16[1024,12,48]{0,2,1:T(8,128)(2,1)S(1)} %slice.241, bf16[1024,12,8]{0,2,1:T(8,128)(2,1)S(1)} %get-tuple-element.37, bf16[1024,12,8]{0,2,1:T(8,128)(2,1)S(1)} %get-tuple-element.36, bf16[1024,12,64]{0,2,1:T(8,128)(2,1)} %copy-done.13), kind=kOutput, calls=%fused_computation.50 | convolution fusion | flops 828893184 | bytes 28073984 | tf_op jit(solution)/shard_map/qhd,khd->hqk/dot_general | solution.py:52
  350.8 12.3 %fusion = f32[12,512]{1,0:T(8,128)S(1)} fusion(f32[12,512]{1,0:T(8,128)S(1)} %get-tuple-element.110, f32[12,512,1024]{2,1,0:T(8,128)} %get-tuple-element.111, pred[512,1024]{1,0:T(8,128)(4,1)S(1)} %copy-done.15), kind=kLoop, calls=%fused_computation.12 | loop fusion | flops 25159680 | bytes 25739264 | tf_op jit(solution)/shard_map/reduce_sum | solution.py:289
  366.2 9.5 fusion.35
  375.7 18.6 %multiply_reduce_fusion.1 = (f32[12,512]{1,0:T(8,128)S(1)}, f32[12,512,1024]{2,1,0:T(8,128)}) fusion(f32[12,512]{1,0:T(8,128)S(1)} %log_add_fusion.1, f32[12,512,1024]{2,1,0:T(8,128)} %get-tuple-element.111, pred[512,1024]{1,0:T(8,128)(4,1)S(1)} %copy-done.15, bf16[512,12,64]{0,2,1:T(8,128)(2,1)} %bitcast.287, f32[1024,3,12,64]{0,3,2,1:T(8,128)} %bitcast.274), kind=kOutput, calls=%fused_computation.4 | convolution fusion | flops 836757504 | bytes 53264384 | tf_op jit(solution)/shard_map/qhd,khd->hqk/dot_general | solution.py:342
  394.3 41.9 %multiply_convert_fusion = (bf16[12,512,1024]{2,1,0:T(8,128)(2,1)}, bf16[12,512,1024]{2,1,0:T(8,128)(2,1)}) fusion(f32[12,512,1024]{2,1,0:T(8,128)} %get-tuple-element.116, f32[12,512]{1,0:T(8,128)S(1)} %copy-done.41, f32[12,512]{1,0:T(8,128)S(1)} %log_add_fusion, f32[12,512,1024]{2,1,0:T(8,128)} %get-tuple-element.109, pred[512,1024]{1,0:T(8,128)(4,1)S(1)} %copy-done.18, ...), kind=kLoop, calls=%fused_computation | loop fusion | flops 75497472 | bytes 126976000 | tf_op jit(solution)/shard_map/convert_element_type | solution.py:353
  436.1 8.6 multiply_bitcast_fusion.2
  444.8 9.1 fusion.46
  453.9 8.5 multiply_bitcast_fusion.1
  465.3 15.1 %add_bitcast_fusion = bf16[1024,1,12,64]{0,3,2,1:T(8,128)(2,1)} fusion(f32[12,64,1024]{2,1,0:T(8,128)} %fusion.5, bf16[512,12,64]{0,2,1:T(8,128)(2,1)} %bitcast.288, f32[12,512]{1,0:T(8,128)S(1)} %log_add_fusion.1, f32[12,512,1024]{2,1,0:T(8,128)} %get-tuple-element.111, pred[512,1024]{1,0:T(8,128)(4,1)} %get-tuple-element.104), kind=kOutput, calls=%fused_computation.74 | convolution fusion | flops 832045056 | bytes 31219712 | tf_op jit(solution)/shard_map/hqk,qhd->khd/dot_general | solution.py:345
  480.4 4.4 multiply_bitcast_fusion
  492.6 5.6 fusion.128
  498.2 4.8 convolution_convert_fusion.2
  516.6 5.1 collective-permute-done.37.refs_2_
  523.3 144.7 %assemble.6 = bf16[768,3072]{1,0:T(8,128)(2,1)} custom-call(s32[3]{0:T(128)} %pad_add_fusion.ids_ref, bf16[192,3072]{1,0:T(8,128)(2,1)} %shard_ref.6, bf16[3,48,1536]{2,1,0:T(8,128)(2,1)} %pad_maximum_fusion.5.refs_0_, bf16[3,48,1536]{2,1,0:T(8,128)(2,1)} %collective-permute-done.26.refs_1_, bf16[3,48,1536]{2,1,0:T(8,128)(2,1)} %collective-permute-done.27.refs_2_, ...), custom_call_target="tpu_custom_call" | custom-call | tf_op jit(solution)/shard_map/assemble/pallas_call | solution.py:120
  668.1 37.5 %multiply_convert_fusion.2 = (bf16[1024,3072]{1,0:T(8,128)(2,1)S(1)}, f32[1024,3072]{1,0:T(8,128)}, f32[1024,3072]{1,0:T(8,128)}) fusion(f32[3072]{0:T(1024)S(1)} %copy-done.60, bf16[768,3072]{1,0:T(8,128)(2,1)} %assemble.6, f32[1024,768]{1,0:T(8,128)S(1)} %copy-done.4, f32[768]{0:T(1024)S(1)} %copy-done.65, f32[768]{0:T(1024)S(1)} %copy-done.57, ...), kind=kOutput, calls=%fused_computation.32 | convolution fusion | flops 5043388416 | bytes 39348224 | tf_op jit(solution)/shard_map/dot_general | solution.py:308
  705.6 7.0 convolution_convert_fusion
  712.7 144.7 %assemble.7 = bf16[3072,768]{1,0:T(8,128)(2,1)} custom-call(s32[3]{0:T(128)} %pad_add_fusion.ids_ref, bf16[768,768]{1,0:T(8,128)(2,1)} %shard_ref.7, bf16[3,192,384]{2,1,0:T(8,128)(2,1)} %pad_maximum_fusion.6.refs_0_, bf16[3,192,384]{2,1,0:T(8,128)(2,1)} %collective-permute-done.36.refs_1_, bf16[3,192,384]{2,1,0:T(8,128)(2,1)} %collective-permute-done.37.refs_2_, ...), custom_call_target="tpu_custom_call" | custom-call | tf_op jit(solution)/shard_map/assemble/pallas_call | solution.py:120
  857.5 18.8 %convert_reduce_fusion = (f32[3072]{0:T(1024)S(1)}, bf16[1024,3072]{1,0:T(8,128)(2,1)}) fusion(f32[1024,3072]{1,0:T(8,128)} %get-tuple-element.31, bf16[3072,768]{1,0:T(8,128)(2,1)} %assemble.7, bf16[1024,768]{1,0:T(8,128)(2,1)} %get-tuple-element.43, f32[1024,3072]{1,0:T(8,128)} %get-tuple-element.112, f32[3072]{0:T(1024)S(1)} %copy-done.60), kind=kOutput, calls=%fused_computation.29 | convolution fusion | flops 4885312512 | bytes 37773312 | tf_op jit(solution)/shard_map/te,fe->tf/dot_general | solution.py:322
  876.3 8.6 convolution_convert_fusion.1
  884.9 11.0 %multiply_reduce_fusion.2 = (f32[768]{0:T(1024)S(1)}, f32[1024]{0:T(1024)S(1)}, f32[1024]{0:T(1024)S(1)}, f32[768]{0:T(1024)S(1)}, f32[768]{0:T(1024)S(1)}, /*index=5*/f32[768]{0:T(1024)S(1)}, f32[1024,768]{1,0:T(8,128)}) fusion(f32[1024,768]{1,0:T(8,128)S(1)} %copy-done.4, f32[1024]{0:T(1024)S(1)} %copy-done.56, f32[1024]{0:T(1024)S(1)} %copy-done.53, ...), kind=kOutput, calls=%fused_computation.69 | convolution fusion | flops 4842842112 | bytes 20482048 | tf_op jit(solution)/shard_map/tf,df->td/dot_general | solution.py:326
  901.3 8.6 add_add_fusion.3
  933.9 6.2 collective-permute-done.51
  941.5 8.9 collective-permute-done.53
  951.9 4.5 collective-permute-done.52
  957.4 5.0 collective-permute-done.54
  982.1 6.9 collective-permute-done.81
  991.1 4.2 collective-permute-done.96
  997.6 7.7 collective-permute-done.98
  1007.4 6.9 collective-permute-done.83
  1016.3 4.8 collective-permute-done.82
  1021.1 6.6 collective-permute-done.84
  1031.6 3.7 collective-permute-done.99
  1050.9 7.4 collective-permute-done.101
  1061.5 8.7 collective-permute-done.86
  (507 shorter events, 209.8 us)
Async XLA Ops:
  6.4 25.9 %collective-permute-start.2 = (bf16[24,128]{1,0:T(8,128)(2,1)S(1)}, bf16[24,128]{1,0:T(8,128)(2,1)S(1)}, u32[]{:S(2)}, u32[]{:S(2)}) collective-permute-start(bf16[24,128]{1,0:T(8,128)(2,1)S(1)} %bitcast.316), channel_id=1, source_target_pairs={{0,3},{1,2},{2,1},{3,0},{4,7},{5,6},{6,5},{7,4},{8,11},{9,10},{10,... | collective-permute-start | bytes 18440 | tf_op jit(solution)/shard_map/ppermute | solution.py:71
  11.5 21.4 %collective-permute-start.1 = (bf16[24,128]{1,0:T(8,128)(2,1)S(1)}, bf16[24,128]{1,0:T(8,128)(2,1)S(1)}, u32[]{:S(2)}, u32[]{:S(2)}) collective-permute-start(bf16[24,128]{1,0:T(8,128)(2,1)S(1)} %bitcast.317), channel_id=1, source_target_pairs={{0,2},{1,3},{2,0},{3,1},{4,6},{5,7},{6,4},{7,5},{8,10},{9,11},{10,... | collective-permute-start | bytes 18440 | tf_op jit(solution)/shard_map/ppermute | solution.py:71
  11.5 25.2 %collective-permute-start = (bf16[24,128]{1,0:T(8,128)(2,1)S(1)}, bf16[24,128]{1,0:T(8,128)(2,1)S(1)}, u32[]{:S(2)}, u32[]{:S(2)}) collective-permute-start(bf16[24,128]{1,0:T(8,128)(2,1)S(1)} %bitcast.318), channel_id=1, source_target_pairs={{0,1},{1,0},{2,3},{3,2},{4,5},{5,4},{6,7},{7,6},{8,9},{9,8},{10,11... | collective-permute-start | bytes 18440 | tf_op jit(solution)/shard_map/ppermute | solution.py:71
  12.9 24.5 %collective-permute-start.15 = (bf16[48,384]{1,0:T(8,128)(2,1)S(1)}, bf16[48,384]{1,0:T(8,128)(2,1)S(1)}, u32[]{:S(2)}, u32[]{:S(2)}) collective-permute-start(bf16[48,384]{1,0:T(8,128)(2,1)S(1)} %dynamic_slice.235), channel_id=1, source_target_pairs={{0,3},{1,2},{2,1},{3,0},{4,7},{5,6},{6,5},{7,4},{8,11},{9,10},{10,... | collective-permute-start | bytes 110600 | tf_op jit(solution)/shard_map/ppermute | solution.py:71
  16.6 21.5 %collective-permute-start.14 = (bf16[48,384]{1,0:T(8,128)(2,1)S(1)}, bf16[48,384]{1,0:T(8,128)(2,1)S(1)}, u32[]{:S(2)}, u32[]{:S(2)}) collective-permute-start(bf16[48,384]{1,0:T(8,128)(2,1)S(1)} %dynamic_slice.235), channel_id=1, source_target_pairs={{0,2},{1,3},{2,0},{3,1},{4,6},{5,7},{6,4},{7,5},{8,10},{9,11},{10,... | collective-permute-start | bytes 110600 | tf_op jit(solution)/shard_map/ppermute | solution.py:71
  37.4 18.6 %collective-permute-start.3 = (bf16[48,1152]{1,0:T(8,128)(2,1)S(1)}, bf16[48,1152]{1,0:T(8,128)(2,1)}, u32[]{:S(2)}, u32[]{:S(2)}) collective-permute-start(bf16[48,1152]{1,0:T(8,128)(2,1)S(1)} %dynamic_slice.234), channel_id=1, source_target_pairs={{0,1},{1,0},{2,3},{3,2},{4,5},{5,4},{6,7},{7,6},{8,9},{9,8},{10,11... | collective-permute-start | bytes 331784 | tf_op jit(solution)/shard_map/ppermute | solution.py:71
  38.2 20.1 %collective-permute-start.19 = (bf16[3,48,384]{2,1,0:T(8,128)(2,1)S(1)}, bf16[3,48,384]{2,1,0:T(8,128)(2,1)S(1)}, u32[]{:S(2)}, u32[]{:S(2)}) collective-permute-start(bf16[3,48,384]{2,1,0:T(8,128)(2,1)S(1)} %pad_maximum_fusion.9.refs_0_), channel_id=1, source_target_pairs={{0,4},{4,0},{8,12},{12,8},{16,20},{20,16},{24,28},{28,24},{1,5},{5... | collective-permute-start | bytes 331784 | tf_op jit(solution)/shard_map/ppermute | solution.py:71
  38.2 20.1 %collective-permute-start.18 = (bf16[3,48,384]{2,1,0:T(8,128)(2,1)S(1)}, bf16[3,48,384]{2,1,0:T(8,128)(2,1)}, u32[]{:S(2)}, u32[]{:S(2)}) collective-permute-start(bf16[3,48,384]{2,1,0:T(8,128)(2,1)S(1)} %pad_maximum_fusion.9.refs_0_), channel_id=1, source_target_pairs={{0,24},{4,28},{8,16},{12,20},{16,8},{20,12},{24,0},{28,4},{1,25},{... | collective-permute-start | bytes 331784 | tf_op jit(solution)/shard_map/ppermute | solution.py:71
  40.9 19.8 %collective-permute-start.17 = (bf16[3,48,384]{2,1,0:T(8,128)(2,1)S(1)}, bf16[3,48,384]{2,1,0:T(8,128)(2,1)}, u32[]{:S(2)}, u32[]{:S(2)}) collective-permute-start(bf16[3,48,384]{2,1,0:T(8,128)(2,1)S(1)} %pad_maximum_fusion.9.refs_0_), channel_id=1, source_target_pairs={{0,16},{4,20},{8,24},{12,28},{16,0},{20,4},{24,8},{28,12},{1,17},{... | collective-permute-start | bytes 331784 | tf_op jit(solution)/shard_map/ppermute | solution.py:71
  44.4 17.4 %collective-permute-start.16 = (bf16[3,48,384]{2,1,0:T(8,128)(2,1)S(1)}, bf16[3,48,384]{2,1,0:T(8,128)(2,1)}, u32[]{:S(2)}, u32[]{:S(2)}) collective-permute-start(bf16[3,48,384]{2,1,0:T(8,128)(2,1)S(1)} %pad_maximum_fusion.9.refs_0_), channel_id=1, source_target_pairs={{0,8},{4,12},{8,0},{12,4},{16,24},{20,28},{24,16},{28,20},{1,9},{5... | collective-permute-start | bytes 331784 | tf_op jit(solution)/shard_map/ppermute | solution.py:71
  58.3 20.2 %collective-permute-start.34 = (bf16[192,384]{1,0:T(8,128)(2,1)}, bf16[192,384]{1,0:T(8,128)(2,1)S(1)}, u32[]{:S(2)}, u32[]{:S(2)}) collective-permute-start(bf16[192,384]{1,0:T(8,128)(2,1)} %dynamic_slice.237), channel_id=1, source_target_pairs={{0,2},{1,3},{2,0},{3,1},{4,6},{5,7},{6,4},{7,5},{8,10},{9,11},{10,... | collective-permute-start | bytes 442376 | tf_op jit(solution)/shard_map/ppermute | solution.py:71
  58.4 21.0 %collective-permute-start.25 = (bf16[48,1536]{1,0:T(8,128)(2,1)}, bf16[48,1536]{1,0:T(8,128)(2,1)S(1)}, u32[]{:S(2)}, u32[]{:S(2)}) collective-permute-start(bf16[48,1536]{1,0:T(8,128)(2,1)} %dynamic_slice.236), channel_id=1, source_target_pairs={{0,3},{1,2},{2,1},{3,0},{4,7},{5,6},{6,5},{7,4},{8,11},{9,10},{10,... | collective-permute-start | bytes 442376 | tf_op jit(solution)/shard_map/ppermute | solution.py:71
  60.8 22.4 %collective-permute-start.24 = (bf16[48,1536]{1,0:T(8,128)(2,1)}, bf16[48,1536]{1,0:T(8,128)(2,1)S(1)}, u32[]{:S(2)}, u32[]{:S(2)}) collective-permute-start(bf16[48,1536]{1,0:T(8,128)(2,1)} %dynamic_slice.236), channel_id=1, source_target_pairs={{0,2},{1,3},{2,0},{3,1},{4,6},{5,7},{6,4},{7,5},{8,10},{9,11},{10,... | collective-permute-start | bytes 442376 | tf_op jit(solution)/shard_map/ppermute | solution.py:71
  61.9 22.2 %collective-permute-start.23 = (bf16[48,1536]{1,0:T(8,128)(2,1)}, bf16[48,1536]{1,0:T(8,128)(2,1)S(1)}, u32[]{:S(2)}, u32[]{:S(2)}) collective-permute-start(bf16[48,1536]{1,0:T(8,128)(2,1)} %dynamic_slice.236), channel_id=1, source_target_pairs={{0,1},{1,0},{2,3},{3,2},{4,5},{5,4},{6,7},{7,6},{8,9},{9,8},{10,11... | collective-permute-start | bytes 442376 | tf_op jit(solution)/shard_map/ppermute | solution.py:71
  65.0 19.9 %collective-permute-start.33 = (bf16[192,384]{1,0:T(8,128)(2,1)}, bf16[192,384]{1,0:T(8,128)(2,1)S(1)}, u32[]{:S(2)}, u32[]{:S(2)}) collective-permute-start(bf16[192,384]{1,0:T(8,128)(2,1)} %dynamic_slice.237), channel_id=1, source_target_pairs={{0,1},{1,0},{2,3},{3,2},{4,5},{5,4},{6,7},{7,6},{8,9},{9,8},{10,11... | collective-permute-start | bytes 442376 | tf_op jit(solution)/shard_map/ppermute | solution.py:71
  78.5 46.8 %collective-permute-start.8 = (bf16[3,48,1152]{2,1,0:T(8,128)(2,1)S(1)}, bf16[3,48,1152]{2,1,0:T(8,128)(2,1)}, u32[]{:S(2)}, u32[]{:S(2)}) collective-permute-start(bf16[3,48,1152]{2,1,0:T(8,128)(2,1)S(1)} %pad_maximum_fusion.8.refs_0_), channel_id=1, source_target_pairs={{0,24},{4,28},{8,16},{12,20},{16,8},{20,12},{24,0},{28,4},{1,25},{... | collective-permute-start | bytes 995336 | tf_op jit(solution)/shard_map/ppermute | solution.py:71
  79.4 46.3 %collective-permute-start.7 = (bf16[3,48,1152]{2,1,0:T(8,128)(2,1)S(1)}, bf16[3,48,1152]{2,1,0:T(8,128)(2,1)}, u32[]{:S(2)}, u32[]{:S(2)}) collective-permute-start(bf16[3,48,1152]{2,1,0:T(8,128)(2,1)S(1)} %pad_maximum_fusion.8.refs_0_), channel_id=1, source_target_pairs={{0,16},{4,20},{8,24},{12,28},{16,0},{20,4},{24,8},{28,12},{1,17},{... | collective-permute-start | bytes 995336 | tf_op jit(solution)/shard_map/ppermute | solution.py:71
  83.2 42.7 %collective-permute-start.6 = (bf16[3,48,1152]{2,1,0:T(8,128)(2,1)S(1)}, bf16[3,48,1152]{2,1,0:T(8,128)(2,1)}, u32[]{:S(2)}, u32[]{:S(2)}) collective-permute-start(bf16[3,48,1152]{2,1,0:T(8,128)(2,1)S(1)} %pad_maximum_fusion.8.refs_0_), channel_id=1, source_target_pairs={{0,8},{4,12},{8,0},{12,4},{16,24},{20,28},{24,16},{28,20},{1,9},{5... | collective-permute-start | bytes 995336 | tf_op jit(solution)/shard_map/ppermute | solution.py:71
  87.2 43.5 %collective-permute-start.9 = (bf16[3,48,1152]{2,1,0:T(8,128)(2,1)S(1)}, bf16[3,48,1152]{2,1,0:T(8,128)(2,1)}, u32[]{:S(2)}, u32[]{:S(2)}) collective-permute-start(bf16[3,48,1152]{2,1,0:T(8,128)(2,1)S(1)} %pad_maximum_fusion.8.refs_0_), channel_id=1, source_target_pairs={{0,4},{4,0},{8,12},{12,8},{16,20},{20,16},{24,28},{28,24},{1,5},{5... | collective-permute-start | bytes 995336 | tf_op jit(solution)/shard_map/ppermute | solution.py:71
  87.6 422.6 %collective-permute-start.29 = (bf16[3,48,1536]{2,1,0:T(8,128)(2,1)}, bf16[3,48,1536]{2,1,0:T(8,128)(2,1)}, u32[]{:S(2)}, u32[]{:S(2)}) collective-permute-start(bf16[3,48,1536]{2,1,0:T(8,128)(2,1)} %pad_maximum_fusion.5.refs_0_), channel_id=1, source_target_pairs={{0,4},{4,0},{8,12},{12,8},{16,20},{20,16},{24,28},{28,24},{1,5},{5... | collective-permute-start | bytes 1327112 | tf_op jit(solution)/shard_map/ppermute | solution.py:71
  130.7 380.4 %collective-permute-start.28 = (bf16[3,48,1536]{2,1,0:T(8,128)(2,1)}, bf16[3,48,1536]{2,1,0:T(8,128)(2,1)}, u32[]{:S(2)}, u32[]{:S(2)}) collective-permute-start(bf16[3,48,1536]{2,1,0:T(8,128)(2,1)} %pad_maximum_fusion.5.refs_0_), channel_id=1, source_target_pairs={{0,24},{4,28},{8,16},{12,20},{16,8},{20,12},{24,0},{28,4},{1,25},{... | collective-permute-start | bytes 1327112 | tf_op jit(solution)/shard_map/ppermute | solution.py:71
  132.5 379.5 %collective-permute-start.27 = (bf16[3,48,1536]{2,1,0:T(8,128)(2,1)}, bf16[3,48,1536]{2,1,0:T(8,128)(2,1)}, u32[]{:S(2)}, u32[]{:S(2)}) collective-permute-start(bf16[3,48,1536]{2,1,0:T(8,128)(2,1)} %pad_maximum_fusion.5.refs_0_), channel_id=1, source_target_pairs={{0,16},{4,20},{8,24},{12,28},{16,0},{20,4},{24,8},{28,12},{1,17},{... | collective-permute-start | bytes 1327112 | tf_op jit(solution)/shard_map/ppermute | solution.py:71
  133.4 378.6 %collective-permute-start.26 = (bf16[3,48,1536]{2,1,0:T(8,128)(2,1)}, bf16[3,48,1536]{2,1,0:T(8,128)(2,1)}, u32[]{:S(2)}, u32[]{:S(2)}) collective-permute-start(bf16[3,48,1536]{2,1,0:T(8,128)(2,1)} %pad_maximum_fusion.5.refs_0_), channel_id=1, source_target_pairs={{0,8},{4,12},{8,0},{12,4},{16,24},{20,28},{24,16},{28,20},{1,9},{5... | collective-permute-start | bytes 1327112 | tf_op jit(solution)/shard_map/ppermute | solution.py:71
  134.3 378.3 %collective-permute-start.38 = (bf16[3,192,384]{2,1,0:T(8,128)(2,1)}, bf16[3,192,384]{2,1,0:T(8,128)(2,1)}, u32[]{:S(2)}, u32[]{:S(2)}) collective-permute-start(bf16[3,192,384]{2,1,0:T(8,128)(2,1)} %pad_maximum_fusion.6.refs_0_), channel_id=1, source_target_pairs={{0,24},{4,28},{8,16},{12,20},{16,8},{20,12},{24,0},{28,4},{1,25},{... | collective-permute-start | bytes 1327112 | tf_op jit(solution)/shard_map/ppermute | solution.py:71
  521.7 190.9 %collective-permute-start.39 = (bf16[3,192,384]{2,1,0:T(8,128)(2,1)}, bf16[3,192,384]{2,1,0:T(8,128)(2,1)}, u32[]{:S(2)}, u32[]{:S(2)}) collective-permute-start(bf16[3,192,384]{2,1,0:T(8,128)(2,1)} %pad_maximum_fusion.6.refs_0_), channel_id=1, source_target_pairs={{0,4},{4,0},{8,12},{12,8},{16,20},{20,16},{24,28},{28,24},{1,5},{5... | collective-permute-start | bytes 1327112 | tf_op jit(solution)/shard_map/ppermute | solution.py:71
  522.3 190.4 %collective-permute-start.42 = (bf16[3,192,384]{2,1,0:T(8,128)(2,1)}, bf16[3,192,384]{2,1,0:T(8,128)(2,1)}, u32[]{:S(2)}, u32[]{:S(2)}) collective-permute-start(bf16[3,192,384]{2,1,0:T(8,128)(2,1)} %collective-permute-done.38.refs_3_), channel_id=1, source_target_pairs={{0,4},{4,0},{8,12},{12,8},{16,20},{20,16},{24,28},{28,24},{1,5},{5... | collective-permute-start | bytes 1327112 | tf_op jit(solution)/shard_map/ppermute | solution.py:71
  522.3 190.4 %collective-permute-start.41 = (bf16[3,192,384]{2,1,0:T(8,128)(2,1)}, bf16[3,192,384]{2,1,0:T(8,128)(2,1)}, u32[]{:S(2)}, u32[]{:S(2)}) collective-permute-start(bf16[3,192,384]{2,1,0:T(8,128)(2,1)} %collective-permute-done.37.refs_2_), channel_id=1, source_target_pairs={{0,4},{4,0},{8,12},{12,8},{16,20},{20,16},{24,28},{28,24},{1,5},{5... | collective-permute-start | bytes 1327112 | tf_op jit(solution)/shard_map/ppermute | solution.py:71
  522.8 189.9 %collective-permute-start.40 = (bf16[3,192,384]{2,1,0:T(8,128)(2,1)}, bf16[3,192,384]{2,1,0:T(8,128)(2,1)}, u32[]{:S(2)}, u32[]{:S(2)}) collective-permute-start(bf16[3,192,384]{2,1,0:T(8,128)(2,1)} %collective-permute-done.36.refs_1_), channel_id=1, source_target_pairs={{0,4},{4,0},{8,12},{12,8},{16,20},{20,16},{24,28},{28,24},{1,5},{5... | collective-permute-start | bytes 1327112 | tf_op jit(solution)/shard_map/ppermute | solution.py:71
  522.9 392.0 %collective-permute-start.65 = (bf16[768,384]{1,0:T(8,128)(2,1)}, bf16[768,384]{1,0:T(8,128)(2,1)}, u32[]{:S(2)}, u32[]{:S(2)}) collective-permute-start(bf16[768,384]{1,0:T(8,128)(2,1)} %constant_dynamic-slice_fusion.14), channel_id=1, source_target_pairs={{0,4},{4,0},{8,12},{12,8},{16,20},{20,16},{24,28},{28,24},{1,5},{5... | collective-permute-start | bytes 1769480 | tf_op jit(solution)/shard_map/ppermute | solution.py:71
  712.6 215.7 %collective-permute-start.50 = (bf16[768,1152]{1,0:T(8,128)(2,1)}, bf16[768,1152]{1,0:T(8,128)(2,1)}, u32[]{:S(2)}, u32[]{:S(2)}) collective-permute-start(bf16[768,1152]{1,0:T(8,128)(2,1)} %constant_dynamic-slice_fusion.19), channel_id=1, source_target_pairs={{0,4},{4,0},{8,12},{12,8},{16,20},{20,16},{24,28},{28,24},{1,5},{5... | collective-permute-start | bytes 5308424 | tf_op jit(solution)/shard_map/ppermute | solution.py:71
  896.1 16.4 %collective-permute-start.43 = (f32[72,128]{1,0:T(8,128)S(1)}, f32[72,128]{1,0:T(8,128)S(1)}, u32[]{:S(2)}, u32[]{:S(2)}) collective-permute-start(f32[72,128]{1,0:T(8,128)S(1)} %bitcast.305), channel_id=1, source_target_pairs={{0,4},{4,0},{8,12},{12,8},{16,20},{20,16},{24,28},{28,24},{1,5},{5... | collective-permute-start | bytes 110600 | tf_op jit(solution)/shard_map/ppermute | solution.py:71
  898.3 79.6 %collective-permute-start.95 = (bf16[3072,384]{1,0:T(8,128)(2,1)}, bf16[3072,384]{1,0:T(8,128)(2,1)}, u32[]{:S(2)}, u32[]{:S(2)}) collective-permute-start(bf16[3072,384]{1,0:T(8,128)(2,1)} %constant_dynamic-slice_fusion.4), channel_id=1, source_target_pairs={{0,4},{4,0},{8,12},{12,8},{16,20},{20,16},{24,28},{28,24},{1,5},{5... | collective-permute-start | bytes 7077896 | tf_op jit(solution)/shard_map/ppermute | solution.py:71
  917.5 58.1 %collective-permute-start.80 = (bf16[768,1536]{1,0:T(8,128)(2,1)S(1)}, bf16[768,1536]{1,0:T(8,128)(2,1)S(1)}, u32[]{:S(2)}, u32[]{:S(2)}) collective-permute-start(bf16[768,1536]{1,0:T(8,128)(2,1)S(1)} %copy-done.26), channel_id=1, source_target_pairs={{0,4},{4,0},{8,12},{12,8},{16,20},{20,16},{24,28},{28,24},{1,5},{5... | collective-permute-start | bytes 7077896 | tf_op jit(solution)/shard_map/ppermute | solution.py:71
  931.6 32.2 %collective-permute-start.70 = (bf16[48,384]{1,0:T(8,128)(2,1)S(1)}, bf16[48,384]{1,0:T(8,128)(2,1)S(1)}, u32[]{:S(2)}, u32[]{:S(2)}) collective-permute-start(bf16[48,384]{1,0:T(8,128)(2,1)S(1)} %get-tuple-element.79), channel_id=1, source_target_pairs={{0,1},{1,0},{2,3},{3,2},{4,5},{5,4},{6,7},{7,6},{8,9},{9,8},{10,11... | collective-permute-start | bytes 110600 | tf_op jit(solution)/shard_map/ppermute | solution.py:71
  931.8 32.2 %collective-permute-start.71 = (bf16[48,384]{1,0:T(8,128)(2,1)S(1)}, bf16[48,384]{1,0:T(8,128)(2,1)S(1)}, u32[]{:S(2)}, u32[]{:S(2)}) collective-permute-start(bf16[48,384]{1,0:T(8,128)(2,1)S(1)} %get-tuple-element.80), channel_id=1, source_target_pairs={{0,2},{1,3},{2,0},{3,1},{4,6},{5,7},{6,4},{7,5},{8,10},{9,11},{10,... | collective-permute-start | bytes 110600 | tf_op jit(solution)/shard_map/ppermute | solution.py:71
  971.1 57.0 %collective-permute-start.49 = (f32[72,128]{1,0:T(8,128)S(1)}, f32[72,128]{1,0:T(8,128)S(1)}, u32[]{:S(2)}, u32[]{:S(2)}) collective-permute-start(f32[72,128]{1,0:T(8,128)S(1)} %add_add_fusion.4), channel_id=1, source_target_pairs={{0,3},{1,2},{2,1},{3,0},{4,7},{5,6},{6,5},{7,4},{8,11},{9,10},{10,... | collective-permute-start | bytes 110600 | tf_op jit(solution)/shard_map/ppermute | solution.py:71
  973.0 58.4 %collective-permute-start.48 = (f32[72,128]{1,0:T(8,128)S(1)}, f32[72,128]{1,0:T(8,128)S(1)}, u32[]{:S(2)}, u32[]{:S(2)}) collective-permute-start(f32[72,128]{1,0:T(8,128)S(1)} %add_add_fusion.4), channel_id=1, source_target_pairs={{0,2},{1,3},{2,0},{3,1},{4,6},{5,7},{6,4},{7,5},{8,10},{9,11},{10,... | collective-permute-start | bytes 110600 | tf_op jit(solution)/shard_map/ppermute | solution.py:71
  974.9 64.4 %collective-permute-start.47 = (f32[72,128]{1,0:T(8,128)S(1)}, f32[72,128]{1,0:T(8,128)S(1)}, u32[]{:S(2)}, u32[]{:S(2)}) collective-permute-start(f32[72,128]{1,0:T(8,128)S(1)} %add_add_fusion.4), channel_id=1, source_target_pairs={{0,1},{1,0},{2,3},{3,2},{4,5},{5,4},{6,7},{7,6},{8,9},{9,8},{10,11... | collective-permute-start | bytes 110600 | tf_op jit(solution)/shard_map/ppermute | solution.py:71
  976.7 12.2 %collective-permute-start.81 = (bf16[2,2,48,1536]{3,2,0,1:T(8,128)(2,1)S(1)}, bf16[2,2,48,1536]{3,2,0,1:T(8,128)(2,1)S(1)}, u32[]{:S(2)}, u32[]{:S(2)}) collective-permute-start(bf16[2,2,48,1536]{3,2,0,1:T(8,128)(2,1)S(1)} %bitcast.293), channel_id=1, source_target_pairs={{0,8},{4,12},{8,0},{12,4},{16,24},{20,28},{24,16},{28,20},{1,9},{5... | collective-permute-start | bytes 1769480 | tf_op jit(solution)/shard_map/ppermute | solution.py:71
  980.7 14.6 %collective-permute-start.96 = (bf16[2,2,192,384]{3,2,0,1:T(8,128)(2,1)S(1)}, bf16[2,2,192,384]{3,2,0,1:T(8,128)(2,1)S(1)}, u32[]{:S(2)}, u32[]{:S(2)}) collective-permute-start(bf16[2,2,192,384]{3,2,0,1:T(8,128)(2,1)S(1)} %bitcast.295), channel_id=1, source_target_pairs={{0,8},{4,12},{8,0},{12,4},{16,24},{20,28},{24,16},{28,20},{1,9},{5... | collective-permute-start | bytes 1769480 | tf_op jit(solution)/shard_map/ppermute | solution.py:71
  989.0 16.3 %collective-permute-start.98 = (bf16[2,2,192,384]{3,2,0,1:T(8,128)(2,1)S(1)}, bf16[2,2,192,384]{3,2,0,1:T(8,128)(2,1)S(1)}, u32[]{:S(2)}, u32[]{:S(2)}) collective-permute-start(bf16[2,2,192,384]{3,2,0,1:T(8,128)(2,1)S(1)} %bitcast.296), channel_id=1, source_target_pairs={{0,16},{4,20},{8,24},{12,28},{16,0},{20,4},{24,8},{28,12},{1,17},{... | collective-permute-start | bytes 1769480 | tf_op jit(solution)/shard_map/ppermute | solution.py:71
  995.3 19.0 %collective-permute-start.83 = (bf16[2,2,48,1536]{3,2,0,1:T(8,128)(2,1)S(1)}, bf16[2,2,48,1536]{3,2,0,1:T(8,128)(2,1)S(1)}, u32[]{:S(2)}, u32[]{:S(2)}) collective-permute-start(bf16[2,2,48,1536]{3,2,0,1:T(8,128)(2,1)S(1)} %bitcast.294), channel_id=1, source_target_pairs={{0,16},{4,20},{8,24},{12,28},{16,0},{20,4},{24,8},{28,12},{1,17},{... | collective-permute-start | bytes 1769480 | tf_op jit(solution)/shard_map/ppermute | solution.py:71
  1005.3 22.6 %collective-permute-start.97 = (bf16[2,192,384]{2,1,0:T(8,128)(2,1)S(1)}, bf16[2,192,384]{2,1,0:T(8,128)(2,1)S(1)}, u32[]{:S(2)}, u32[]{:S(2)}) collective-permute-start(bf16[2,192,384]{2,1,0:T(8,128)(2,1)S(1)} %dynamic-slice_bitcast_fusion.1), channel_id=1, source_target_pairs={{0,16},{4,20},{8,24},{12,28},{16,0},{20,4},{24,8},{28,12},{1,17},{... | collective-permute-start | bytes 884744 | tf_op jit(solution)/shard_map/ppermute | solution.py:71
  1044.1 14.2 %collective-permute-start.101 = (bf16[192,384]{1,0:T(8,128)(2,1)S(1)}, bf16[192,384]{1,0:T(8,128)(2,1)S(1)}, u32[]{:S(2)}, u32[]{:S(2)}) collective-permute-start(bf16[192,384]{1,0:T(8,128)(2,1)S(1)} %get-tuple-element.65), channel_id=1, source_target_pairs={{0,2},{1,3},{2,0},{3,1},{4,6},{5,7},{6,4},{7,5},{8,10},{9,11},{10,... | collective-permute-start | bytes 442376 | tf_op jit(solution)/shard_map/ppermute | solution.py:71
  1058.3 13.4 %collective-permute-start.87 = (bf16[48,1536]{1,0:T(8,128)(2,1)S(1)}, bf16[48,1536]{1,0:T(8,128)(2,1)S(1)}, u32[]{:S(2)}, u32[]{:S(2)}) collective-permute-start(bf16[48,1536]{1,0:T(8,128)(2,1)S(1)} %get-tuple-element.69), channel_id=1, source_target_pairs={{0,3},{1,2},{2,1},{3,0},{4,7},{5,6},{6,5},{7,4},{8,11},{9,10},{10,... | collective-permute-start | bytes 442376 | tf_op jit(solution)/shard_map/ppermute | solution.py:71
  1059.5 12.6 %collective-permute-start.62 = (bf16[48,1152]{1,0:T(8,128)(2,1)S(1)}, bf16[48,1152]{1,0:T(8,128)(2,1)S(1)}, u32[]{:S(2)}, u32[]{:S(2)}) collective-permute-start(bf16[48,1152]{1,0:T(8,128)(2,1)S(1)} %collective-permute-done.58.refs_1_), channel_id=1, source_target_pairs={{0,4},{4,0},{8,12},{12,8},{16,20},{20,16},{24,28},{28,24},{1,5},{5... | collective-permute-start | bytes 331784 | tf_op jit(solution)/shard_map/ppermute | solution.py:71
  1059.6 14.3 %collective-permute-start.106 = (bf16[192,384]{1,0:T(8,128)(2,1)S(1)}, bf16[192,384]{1,0:T(8,128)(2,1)S(1)}, u32[]{:S(2)}, u32[]{:S(2)}) collective-permute-start(bf16[192,384]{1,0:T(8,128)(2,1)S(1)} %fusion.58.refs_0_), channel_id=1, source_target_pairs={{0,4},{4,0},{8,12},{12,8},{16,20},{20,16},{24,28},{28,24},{1,5},{5... | collective-permute-start | bytes 442376 | tf_op jit(solution)/shard_map/ppermute | solution.py:71
  1060.1 15.3 %collective-permute-start.105 = (bf16[192,384]{1,0:T(8,128)(2,1)S(1)}, bf16[192,384]{1,0:T(8,128)(2,1)S(1)}, u32[]{:S(2)}, u32[]{:S(2)}) collective-permute-start(bf16[192,384]{1,0:T(8,128)(2,1)S(1)} %fusion.58.refs_0_), channel_id=1, source_target_pairs={{0,24},{4,28},{8,16},{12,20},{16,8},{20,12},{24,0},{28,4},{1,25},{... | collective-permute-start | bytes 442376 | tf_op jit(solution)/shard_map/ppermute | solution.py:71
  (142 other events, 2701.2 us)

commit v2 on v0

v2 whole, which is shorter than its diff:
```python
import functools

import jax
import jax.numpy as jnp
from jax import lax
from jax.experimental import pallas as pl
from jax.experimental.pallas import tpu as pltpu
from jax.sharding import PartitionSpec as P

D = 768
H = 12
HD = 64
ROT = 16
WIDE = 384
LANES = 128
F32, BF16 = jnp.float32, jnp.bfloat16
norm_eps = 1e-05


def compiler_params(mib):
    return pltpu.CompilerParams(vmem_limit_bytes=mib * 2**20)


VMEM = pl.BlockSpec(memory_space=pltpu.VMEM)
SMEM = pl.BlockSpec(memory_space=pltpu.SMEM)


def swap(value, axis, bit):
    size = lax.axis_size(axis)
    return lax.ppermute(value, axis, [(i, i ^ bit) for i in range(size)])


def place_ids():
    rep = lax.axis_index("rep")
    return lax.axis_index("shard"), (rep // 2) % 4, rep % 2


def gather_far(piece):
    return jnp.stack([swap(piece, "shard", k) for k in (1, 2, 3)])


def gather_near(far):
    parts = jnp.stack([far] + [swap(far, "rep", j * 2) for j in (1, 2, 3)])
    return parts, swap(parts, "rep", 1)


def pair(left, right):
    return left.astype(F32) + right.astype(F32)


def reduce_pack(send, keep):
    z, q, c = place_ids()
    y_bit, x_bit = q // 2, q % 2
    rows = keep.shape[2]
    got = swap(send, "rep", 1)
    one = pair(keep, got).astype(BF16).reshape(4, 2, 2, rows, WIDE)

    def halves(block, bit, axis):
        mine = lax.dynamic_index_in_dim(block, bit, axis, keepdims=False)
        theirs = lax.dynamic_index_in_dim(block, 1 - bit, axis, keepdims=False)
        return mine, theirs

    low_mine, low_theirs = halves(one[:2], x_bit, 2)
    high_mine, high_theirs = halves(one[2:], y_bit, 1)
    low = pair(low_mine, swap(low_theirs, "rep", 2)).astype(BF16)
    high = pair(high_mine, swap(high_theirs, "rep", 4)).astype(BF16)
    low_mine, low_theirs = halves(low, y_bit, 1)
    high_mine, high_theirs = halves(high, x_bit, 1)
    low_got = swap(low_theirs, "rep", 4)
    high_got = swap(high_theirs, "rep", 2)
    two = jnp.concatenate([pair(low_mine, low_got), pair(high_mine, high_got)]).astype(BF16)
    pieces = [lax.dynamic_index_in_dim(two, z ^ k, 0, keepdims=False) for k in range(4)]
    got = [swap(pieces[k], "shard", k) for k in (1, 2, 3)]
    three = (pair(pieces[0], got[0]) + pair(got[1], got[2])).astype(BF16)
    bit = 8
    while bit < lax.axis_size("rep"):
        three = pair(three, swap(three, "rep", bit)).astype(BF16)
        bit *= 2
    parts = jnp.stack([three] + [swap(three, "rep", j * 2) for j in (1, 2, 3)])
    return parts, swap(parts, "rep", 1)


def sum_small(vector):
    bit = 1
    while bit < lax.axis_size("rep"):
        if bit not in (2, 4):
            vector = vector + swap(vector, "rep", bit)
        bit *= 2
    vector = (vector + swap(vector, "rep", 2)) + (swap(vector, "rep", 4) + swap(vector, "rep", 6))
    return (vector + swap(vector, "shard", 1)) + (swap(vector, "shard", 2) + swap(vector, "shard", 3))


def pack(vectors):
    flat = jnp.concatenate([v.reshape(-1) for v in vectors])
    fill = -flat.shape[0] % 1024
    return jnp.concatenate([flat, jnp.zeros((fill,), flat.dtype)]).reshape(-1, LANES)


def gather_small(vectors):
    packed = pack(vectors)
    z = lax.axis_index("shard")
    near = jnp.stack([packed] + [swap(packed, "shard", k) for k in (1, 2, 3)])
    rows = jnp.stack(
        [lax.dynamic_index_in_dim(near, z ^ i, 0, keepdims=False) for i in range(4)]
    ).reshape(4, -1)
    out, at = [], 0
    for v in vectors:
        out.append(rows[:, at : at + v.shape[0]].reshape(-1).astype(F32))
        at += v.shape[0]
    return out


def assemble_body(plan, ids_ref, *refs):
    count = len(plan)
    shards, (parts_ref, other_ref), outs = refs[:count], refs[count : count + 2], refs[count + 2 :]
    z, q, c = ids_ref[0], ids_ref[1], ids_ref[2]
    for shard_ref, out_ref, (rows, part, first, blocks) in zip(shards, outs, plan):
        half = blocks * WIDE
        out_ref[pl.ds(pl.multiple_of(z * rows, rows), rows), :] = shard_ref[...]
        for h, pieces in ((c, parts_ref), (1 - c, other_ref)):
            for j in range(4):
                for k in (1, 2, 3):
                    row = pl.multiple_of((z ^ k) * rows + (q ^ j) * part, part)
                    for b in range(blocks):
                        col = pl.multiple_of(h * half + b * WIDE, WIDE)
                        at = first + b * part
                        out_ref[pl.ds(row, part), pl.ds(col, WIDE)] = pieces[j, k - 1, at : at + part, :]


def assemble(ids, shards, plan, parts, other):
    shapes = [
        jax.ShapeDtypeStruct((4 * rows, 2 * blocks * WIDE), BF16) for rows, _, _, blocks in plan
    ]
    return pl.pallas_call(
        functools.partial(assemble_body, plan),
        out_shape=shapes,
        in_specs=[SMEM] + [VMEM] * (len(shards) + 2),
        out_specs=[VMEM] * len(shards),
        compiler_params=compiler_params(40),
        name="assemble",
    )(ids, *shards, parts, other)


def place_body(plan, ids_ref, parts_ref, other_ref, *outs):
    q, c = ids_ref[1], ids_ref[2]
    for out_ref, (rows, part, first, blocks) in zip(outs, plan):
        half = blocks * WIDE
        for h, pieces in ((c, parts_ref), (1 - c, other_ref)):
            for j in range(4):
                row = pl.multiple_of((q ^ j) * part, part)
                for b in range(blocks):
                    col = pl.multiple_of(h * half + b * WIDE, WIDE)
                    at = first + b * part
                    out_ref[pl.ds(row, part), pl.ds(col, WIDE)] = pieces[j, at : at + part, :].astype(F32)


def place(ids, plan, parts, other):
    shapes = [jax.ShapeDtypeStruct((rows, 2 * blocks * WIDE), F32) for rows, _, _, blocks in plan]
    return pl.pallas_call(
        functools.partial(place_body, plan),
        out_shape=shapes,
        in_specs=[SMEM, VMEM, VMEM],
        out_specs=[VMEM] * len(plan),
        compiler_params=compiler_params(40),
        name="place",
    )(ids, parts, other)


def dot(left, right, left_dim=1, right_dim=0):
    return lax.dot_general(
        left, right, (((left_dim,), (right_dim,)), ((), ())), preferred_element_type=F32
    )


def turn(values, cosine, early, late):
    width = values.shape[1]
    return (
        values * cosine
        + pltpu.roll(values, width - ROT // 2, 1) * early
        + pltpu.roll(values, ROT // 2, 1) * late
    )


def qkv_body(x_ref, w_ref, bias_ref, cos_ref, early_ref, late_ref, out_ref):
    values = dot(x_ref[...], w_ref[...]) + bias_ref[...]

    @pl.when(pl.program_id(0) < 4)
    def rotate_block():
        for b in range(WIDE // LANES):
            cols = slice(b * LANES, (b + 1) * LANES)
            out_ref[:, cols] = turn(
                values[:, cols], cos_ref[...], early_ref[...], late_ref[...]
            ).astype(BF16)

    @pl.when(pl.program_id(0) >= 4)
    def plain_block():
        out_ref[...] = values.astype(BF16)


def qkv_call(first_b, weight, bias, tables):
    tokens = first_b.shape[0]
    whole = lambda r, c: pl.BlockSpec((r, c), lambda i: (0, 0))
    return pl.pallas_call(
        qkv_body,
        grid=(3 * D // WIDE,),
        out_shape=jax.ShapeDtypeStruct((tokens, 3 * D), BF16),
        in_specs=[
            whole(tokens, D),
            pl.BlockSpec((D, WIDE), lambda i: (0, i)),
            pl.BlockSpec((1, WIDE), lambda i: (0, i)),
        ]
        + [whole(tokens, LANES)] * 3,
        out_specs=pl.BlockSpec((tokens, WIDE), lambda i: (0, i)),
        compiler_params=compiler_params(40),
        name="qkv",
    )(first_b, weight, bias, *tables)


def attention_body(
    q_ref, k_ref, v_ref, cot_ref, w_ref, seg_col_ref, seg_row_ref, cos_ref, early_ref, late_ref,
    mixed_ref, grad_ref, mask_ref, key_t_ref, value_t_ref,
):
    tokens = q_ref.shape[0]
    step = min(256, tokens)

    @pl.when(pl.program_id(0) == 0)
    def make_mask():
        for first in range(0, tokens, step):
            rows = first + lax.broadcasted_iota(jnp.int32, (step, tokens), 0)
            cols = lax.broadcasted_iota(jnp.int32, (step, tokens), 1)
            same = seg_col_ref[first : first + step, :] == seg_row_ref[...]
            mask_ref[first : first + step, :] = jnp.where(same & (cols <= rows), 0.0, -1e30)

    out_grad = dot(cot_ref[...], w_ref[...], 1, 1).astype(BF16)
    lane = lax.broadcasted_iota(jnp.int32, (tokens, LANES), 1)
    query_t = q_ref[...].astype(F32).T.astype(BF16)
    out_grad_t = out_grad.astype(F32).T.astype(BF16)
    nothing = jnp.zeros((tokens, LANES), BF16)
    keys = k_ref[...] * BF16(HD**-0.5)
    heads = []
    for h in range(2):
        here = (lane // HD) == h
        heads.append((jnp.where(here, keys, nothing), jnp.where(here, v_ref[...], nothing)))
    key_t_ref[...] = jnp.zeros_like(key_t_ref)
    value_t_ref[...] = jnp.zeros_like(value_t_ref)
    for first in range(0, tokens, step):
        last = first + step
        block = slice(first, last)
        mixed = jnp.zeros((step, LANES), F32)
        query_grad = jnp.zeros((step, LANES), F32)
        for h in range(2):
            key, value = heads[h][0][:last], heads[h][1][:last]
            rows = slice(h * HD, (h + 1) * HD)
            scores = dot(q_ref[block, :], key, 1, 1) + mask_ref[block, :last]
            expo = jnp.exp(scores - jnp.max(scores, axis=1, keepdims=True))
            probs = expo * (1.0 / jnp.sum(expo, axis=1, keepdims=True))
            probs_b = probs.astype(BF16)
            mixed += dot(probs_b, value)
            probs_grad = dot(out_grad[block], value, 1, 1)
            weighted = probs_grad * probs
            scores_grad = (weighted - probs * jnp.sum(weighted, axis=1, keepdims=True)).astype(BF16)
            query_grad += dot(scores_grad, key)
            key_t_ref[rows, :last] += dot(query_t[rows, block], scores_grad)
            value_t_ref[rows, :last] += dot(out_grad_t[rows, block], probs_b)
        mixed_ref[block, :] = mixed.astype(BF16)
        grad_ref[0, block, :] = turn(
            query_grad, cos_ref[block, :], -early_ref[block, :], -late_ref[block, :]
        ).astype(BF16)
    grad_ref[1, :, :] = turn(
        key_t_ref[...].T * HD**-0.5, cos_ref[...], -early_ref[...], -late_ref[...]
    ).astype(BF16)
    grad_ref[2, :, :] = value_t_ref[...].T.astype(BF16)


def attention_call(qkv_b, cot_b, out_weight, segments, tables):
    tokens = qkv_b.shape[0]
    pairs = D // LANES
    whole = lambda r, c: pl.BlockSpec((r, c), lambda i: (0, 0))
    part = lambda n: pl.BlockSpec((tokens, LANES), lambda i: (0, n * pairs + i))
    return pl.pallas_call(
        attention_body,
        grid=(pairs,),
        out_shape=[
            jax.ShapeDtypeStruct((tokens, D), BF16),
            jax.ShapeDtypeStruct((3, tokens, D), BF16),
        ],
        in_specs=[
            part(0),
            part(1),
            part(2),
            whole(tokens, D),
            pl.BlockSpec((LANES, D), lambda i: (i, 0)),
            whole(tokens, 1),
            whole(1, tokens),
        ]
        + [whole(tokens, LANES)] * 3,
        out_specs=[
            pl.BlockSpec((tokens, LANES), lambda i: (0, i)),
            pl.BlockSpec((3, tokens, LANES), lambda i: (0, 0, i)),
        ],
        scratch_shapes=[
            pltpu.VMEM((tokens, tokens), F32),
            pltpu.VMEM((LANES, tokens), F32),
            pltpu.VMEM((LANES, tokens), F32),
        ],
        compiler_params=compiler_params(56),
        name="attention",
    )(
        qkv_b, qkv_b, qkv_b, cot_b, out_weight, segments[:, None], segments[None, :], *tables
    )


def qkv_grad_body(grad_ref, first_t_ref, w_ref, mixed_ref, cot_ref, pack_ref, bias_ref, in_ref):
    step = pl.program_id(0)
    grad = grad_ref[0]
    h, b = step // 3, step % 3
    block = dot(first_t_ref[...], grad).astype(BF16).reshape(4, 4, D // 16, WIDE)
    pack_ref[h, :, :, pl.ds(pl.multiple_of(b * (D // 16), D // 16), D // 16), :] = block
    bias_ref[...] = jnp.sum(grad.astype(F32), axis=0, keepdims=True)
    back = dot(grad, w_ref[...], 1, 1)

    @pl.when(step == 0)
    def first_step():
        in_ref[...] = back

    @pl.when(step > 0)
    def later_step():
        in_ref[...] += back

    @pl.when(b == 0)
    def out_part():
        block = dot(mixed_ref[...], cot_ref[...], 0, 0).astype(BF16)
        pack_ref[h, :, :, 3 * (D // 16) :, :] = block.reshape(4, 4, D // 16, WIDE)


def qkv_grad_call(grads, first_t, weight, mixed_b, cot_b):
    tokens = cot_b.shape[0]
    whole = lambda r, c: pl.BlockSpec((r, c), lambda i: (0, 0))
    return pl.pallas_call(
        qkv_grad_body,
        grid=(3 * D // WIDE,),
        out_shape=[
            jax.ShapeDtypeStruct((2, 4, 4, D // 4, WIDE), BF16),
            jax.ShapeDtypeStruct((1, 3 * D), F32),
            jax.ShapeDtypeStruct((tokens, D), F32),
        ],
        in_specs=[
            pl.BlockSpec((1, tokens, WIDE), lambda i: (i // 2, 0, i % 2)),
            whole(D, tokens),
            pl.BlockSpec((D, WIDE), lambda i: (0, i)),
            whole(tokens, D),
            pl.BlockSpec((tokens, WIDE), lambda i: (0, i // 3)),
        ],
        out_specs=[
            pl.BlockSpec((2, 4, 4, D // 4, WIDE), lambda i: (0, 0, 0, 0, 0)),
            pl.BlockSpec((1, WIDE), lambda i: (0, i)),
            whole(tokens, D),
        ],
        compiler_params=compiler_params(56),
        name="qkv_grad",
    )(grads, first_t, weight, mixed_b, cot_b)


def mlp_body(x_ref, x_t_ref, cot_ref, up_ref, down_ref, bias_ref, out_in_ref, back_in_ref, out_ref, back_ref, pack_ref, bias_grad_ref, act_ref, grad_ref):
    step = pl.program_id(0)
    tokens = x_ref.shape[0]
    rows = min(256, tokens)
    total = jnp.zeros((1, WIDE), F32)

    @pl.when(step == 0)
    def first_step():
        out_ref[...] = out_in_ref[...]
        back_ref[...] = back_in_ref[...]

    for first in range(0, tokens, rows):
        block = slice(first, first + rows)
        up = dot(x_ref[block, :], up_ref[...]) + bias_ref[...]
        act_grad = dot(cot_ref[block, :], down_ref[...], 1, 1)
        below = 0.5 + 0.5 * lax.erf(up * (0.5**0.5))
        act = (up * below).astype(BF16)
        slope = below + up * (jnp.exp(-0.5 * up * up) * 0.3989422804014327)
        up_grad = (act_grad * slope).astype(BF16)
        act_ref[block, :] = act
        grad_ref[block, :] = up_grad
        out_ref[block, :] += dot(act, down_ref[...])
        back_ref[block, :] += dot(up_grad, up_ref[...], 1, 1)
        total += jnp.sum(up_grad.astype(F32), axis=0, keepdims=True)
    bias_grad_ref[...] = total
    part = D // 16
    block = dot(x_t_ref[...], grad_ref[...]).astype(BF16).reshape(4, 4, part, WIDE)
    pack_ref[step // 2, :, :, pl.ds(pl.multiple_of((step % 2) * part, part), part), :] = block
    down = dot(act_ref[...], cot_ref[...], 0, 0).astype(BF16)
    for h in range(2):
        pack_ref[h, step, :, 2 * part :, :] = down[:, h * WIDE : (h + 1) * WIDE].reshape(
            4, WIDE // 4, WIDE
        )


def mlp_call(second_b, second_t, cot_b, up_weight, down_weight, bias, out_in, back_in):
    tokens = cot_b.shape[0]
    whole = lambda r, c: pl.BlockSpec((r, c), lambda i: (0, 0))
    return pl.pallas_call(
        mlp_body,
        grid=(4,),
        out_shape=[
            jax.ShapeDtypeStruct((tokens, D), F32),
            jax.ShapeDtypeStruct((tokens, D), F32),
            jax.ShapeDtypeStruct((2, 4, 4, D // 4, WIDE), BF16),
            jax.ShapeDtypeStruct((1, 4 * WIDE), F32),
        ],
        in_specs=[
            whole(tokens, D),
            whole(D, tokens),
            whole(tokens, D),
            pl.BlockSpec((D, WIDE), lambda i: (0, i)),
            pl.BlockSpec((WIDE, D), lambda i: (i, 0)),
            pl.BlockSpec((1, WIDE), lambda i: (0, i)),
            whole(tokens, D),
            whole(tokens, D),
        ],
        out_specs=[
            whole(tokens, D),
            whole(tokens, D),
            pl.BlockSpec((2, 4, 4, D // 4, WIDE), lambda i: (0, 0, 0, 0, 0)),
            pl.BlockSpec((1, WIDE), lambda i: (0, i)),
        ],
        scratch_shapes=[pltpu.VMEM((tokens, WIDE), BF16), pltpu.VMEM((tokens, WIDE), BF16)],
        input_output_aliases={6: 0, 7: 1},
        compiler_params=compiler_params(60),
        name="mlp",
    )(second_b, second_t, cot_b, up_weight, down_weight, bias, out_in, back_in)


def normalize(values):
    centre = values - jnp.mean(values, axis=-1, keepdims=True)
    scale = lax.rsqrt(jnp.mean(centre * centre, axis=-1, keepdims=True) + norm_eps)
    return centre * scale, scale


def norm_back(normed, scale, gain, grad):
    inner = grad * gain
    return scale * (
        inner
        - jnp.mean(inner, axis=-1, keepdims=True)
        - normed * jnp.mean(inner * normed, axis=-1, keepdims=True)
    )


def rotary_tables(segments):
    tokens = segments.shape[0]
    before = jnp.sum((segments[:, None] > segments[None, :]).astype(jnp.int32), axis=1)
    places = jnp.arange(tokens, dtype=jnp.int32) - before
    half = ROT // 2
    lane = jnp.arange(LANES, dtype=jnp.int32) % HD
    freqs = 1.0 / 10000.0 ** ((lane % half).astype(F32) * 2.0 / ROT)
    angles = places.astype(F32)[:, None] * freqs[None, :]
    cosine, sine = jnp.cos(angles), jnp.sin(angles)
    turned, early = (lane < ROT)[None, :], (lane < half)[None, :]
    return (
        jnp.where(turned, cosine, 1.0),
        jnp.where(early, -sine, 0.0),
        jnp.where(turned & ~early, sine, 0.0),
    )


def take(array, row, col, rows, cols):
    return lax.dynamic_slice(array, (row, col), (rows, cols))


def body(
    hidden_in,
    cotangent,
    seg_ids,
    first_gain,
    first_shift,
    second_gain,
    second_shift,
    qkv_weight,
    qkv_bias,
    out_weight,
    out_bias,
    up_weight,
    up_bias,
    down_weight,
    down_bias,
):
    z, q, c = place_ids()
    ids = jnp.stack([z, q, c]).astype(jnp.int32)
    own = qkv_weight.shape[0]
    part = own // 4
    hidden_units = up_weight.shape[1]
    own_hidden = down_weight.shape[0]
    chunks = own_hidden // WIDE
    small = gather_small(
        [first_gain, first_shift, second_gain, second_shift, qkv_bias, out_bias, up_bias, down_bias]
    )
    gain_1, shift_1, gain_2, shift_2, qkv_b0, out_b0, up_b0, down_b0 = small

    attention_piece = jnp.concatenate(
        [take(qkv_weight, q * part, c * 3 * WIDE + b * WIDE, part, WIDE) for b in range(3)]
        + [take(out_weight, q * part, c * WIDE, part, WIDE)]
    )
    attention_plan = ((own, part, 0, 3), (own, part, 3 * part, 1))
    deep = WIDE // 4
    mlp_plan = ((own, part, 0, 2), (WIDE, deep, 2 * part, 1))
    far = gather_far(attention_piece)
    qkv_full, out_full = assemble(
        ids, (qkv_weight, out_weight), attention_plan, *gather_near(far)
    )
    mlp_weights = []
    for j in range(chunks):
        piece = jnp.concatenate(
            [take(up_weight, q * part, (2 * c + b) * own_hidden + j * WIDE, part, WIDE) for b in range(2)]
            + [take(down_weight, j * WIDE + q * deep, c * WIDE, deep, WIDE)]
        )
        piece, far = lax.optimization_barrier((piece, far))
        far = gather_far(piece)
        own_up = up_weight.reshape(own, 4, chunks, WIDE)[:, :, j].reshape(own, 4 * WIDE)
        own_down = down_weight[j * WIDE : (j + 1) * WIDE]
        mlp_weights.append(assemble(ids, (own_up, own_down), mlp_plan, *gather_near(far)))

    normed_1, scale = normalize(hidden_in)
    first_b = (normed_1 * gain_1 + shift_1).astype(BF16)
    second_b = (normed_1 * gain_2 + shift_2).astype(BF16)
    cot_b = cotangent.astype(BF16)
    column_sum = jnp.sum(cotangent, axis=0)
    tables = rotary_tables(seg_ids)

    qkv_b = qkv_call(first_b, qkv_full, qkv_b0[None, :], tables)
    mixed_b, grads = attention_call(qkv_b, cot_b, out_full, seg_ids, tables)
    packed, qkv_bias_g, first_in_grad = qkv_grad_call(grads, first_b.T, qkv_full, mixed_b, cot_b)

    def half_sums(packed):
        send = lax.dynamic_index_in_dim(packed, 1 - c, 0, keepdims=False)
        keep = lax.dynamic_index_in_dim(packed, c, 0, keepdims=False)
        return reduce_pack(send, keep)

    qkv_weight_g, out_weight_g = place(ids, attention_plan, *half_sums(packed))

    attention_out = jnp.dot(mixed_b, out_full, preferred_element_type=F32)
    output = hidden_in + (attention_out + out_b0) + down_b0
    second_in_grad = jnp.zeros(hidden_in.shape, F32)
    second_t = second_b.T
    up_parts, down_parts, bias_parts = [], [], []
    bias_blocks = up_b0.reshape(4, chunks, WIDE)
    for j in range(chunks):
        output, second_in_grad, packed, bias_g = mlp_call(
            second_b,
            second_t,
            cot_b,
            *mlp_weights[j],
            bias_blocks[:, j].reshape(1, 4 * WIDE),
            output,
            second_in_grad,
        )
        up_g, down_g = place(ids, mlp_plan, *half_sums(packed))
        up_parts.append(up_g.reshape(own, 4, WIDE))
        down_parts.append(down_g)
        bias_parts.append(bias_g.reshape(4, WIDE))
    up_weight_g = jnp.stack(up_parts, axis=2).reshape(own, hidden_units)
    down_weight_g = jnp.concatenate(down_parts)
    up_bias_g = jnp.stack(bias_parts, axis=1).reshape(-1)

    input_grad = (
        cotangent
        + norm_back(normed_1, scale, gain_1, first_in_grad)
        + norm_back(normed_1, scale, gain_2, second_in_grad)
    )
    sums = [
        jnp.sum(first_in_grad * normed_1, axis=0),
        jnp.sum(first_in_grad, axis=0),
        jnp.sum(second_in_grad * normed_1, axis=0),
        jnp.sum(second_in_grad, axis=0),
        qkv_bias_g.reshape(-1),
        column_sum,
        up_bias_g,
    ]
    total = sum_small(pack(sums)).reshape(-1)
    summed, at = [], 0
    for s in sums:
        size = s.shape[0] // 4
        summed.append(lax.dynamic_slice(total, (at + z * size,), (size,)))
        at += s.shape[0]
    return (
        output,
        input_grad,
        summed[0],
        summed[1],
        summed[2],
        summed[3],
        qkv_weight_g,
        summed[4],
        out_weight_g,
        summed[5],
        up_weight_g,
        summed[6],
        down_weight_g,
        summed[5],
    )


def solution(mesh):
    tokens = P(("rep", "shard"), None)
    matrix, vector = P("shard", None), P("shard")
    params = (vector,) * 4 + (matrix, vector) * 4
    in_specs = (tokens, tokens, P(("rep", "shard"))) + params
    out_specs = (tokens, tokens) + params
    return jax.shard_map(body, mesh=mesh, in_specs=in_specs, out_specs=out_specs, check_vma=False)
```

time: 968 us -> 496 us (0.51)
  waiting for transfers between devices: 475 us -> 84.8 us
  matrix products: 264 us -> 5.52 us
  Pallas kernels: 0 us -> 153 us
  starting transfers between devices: 0.36 us -> 84.1 us
  blocking collectives: 79.7 us -> 0 us
  local copies, waits for them, and re-layouts: 35.7 us -> 103 us
  other arithmetic: 91.6 us -> 54.1 us
  between operations: 18.4 us -> 2.42 us
    reduce_scatter x4 -> x0, waiting for transfers between devices: 353 us -> none  [the longest x1 165 us: body(): lax.psum_scatter(down_weight_g, 'shard', scatter_dimension=0, tiled=True)]
    dot_general x24 -> x1, matrix products: 264 us -> 5.52 us  [body(): attention_out = jnp.dot(mixed_b, out_full, preferred_element_type=F32)]
    pallas_call x0 -> x11, Pallas kernels: none -> 153 us  [the longest x2 55.4 us: mlp_call(): pl.pallas_call(mlp_body, grid=(4,), out_shape=[jax.ShapeDtypeStruct((toke...]
    ppermute x0 -> x67, waiting for transfers between devices: none -> 84.8 us  [swap(): return lax.ppermute(value, axis, [(i, i ^ bit) for i in range(size)])]
    ppermute x0 -> x67, starting transfers between devices: none -> 84.1 us  [swap(): return lax.ppermute(value, axis, [(i, i ^ bit) for i in range(size)])]
    all_gather x4 -> x0, waiting for transfers between devices: 64.5 us -> none  [the longest x1 64.5 us: body(): lax.all_gather(qkv_weight, 'shard', axis=0, tiled=True)]
    psum x1 -> x0, waiting for transfers between devices: 55 us -> none  [body(): lax.psum((all_owned[0], all_owned[1], all_owned[2], all_owned[3], all_own...]
    unnamed x2 -> x0, blocking collectives: 41.6 us -> none
  transfers between devices with their start and end apart: 9 -> 67, of which waited for: 5 -> 20; matrix products, arithmetic and copies ran while one was open for 39% -> 27% of each run, Pallas kernels for 0% -> 31%
where the time goes in v2:
time: 496 us; the launch traced here: 487 us
  Pallas kernels  153 us (31%)
  local copies, waits for them, and re-layouts  103 us (21%)
  waiting for transfers between devices  84.8 us (17%)
  starting transfers between devices  84.1 us (17%)
  other arithmetic  54.1 us (11%)
  matrix products  5.52 us (1%)
    ppermute x67, waiting for transfers between devices, swap(): return lax.ppermute(value, axis, [(i, i ^ bit) for i in range(size)])  84.8 us
    ppermute x67, starting transfers between devices, swap(): return lax.ppermute(value, axis, [(i, i ^ bit) for i in range(size)])  84.1 us
    pallas_call x2, Pallas kernels, mlp_call(): pl.pallas_call(mlp_body, grid=(4,), out_shape=[jax.ShapeDtypeStruct((toke...  55.4 us
    pallas_call x1, Pallas kernels, attention_call(): pl.pallas_call(attention_body, grid=(pairs,), out_shape=[jax.ShapeDtypeSt...  55.2 us
    unnamed x148, local copies, waits for them, and re-layouts  27.8 us
    pallas_call x1, Pallas kernels, qkv_grad_call(): pl.pallas_call(qkv_grad_body, grid=(3 * D // WIDE,), out_shape=[jax.Shape...  20.9 us
    pallas_call x1, local copies, waits for them, and re-layouts, qkv_grad_call(): pl.pallas_call(qkv_grad_body, grid=(3 * D // WIDE,), out_shape=[jax.Shape...  13.7 us
    pallas_call x1, Pallas kernels, qkv_call(): pl.pallas_call(qkv_body, grid=(3 * D // WIDE,), out_shape=jax.ShapeDtypeS...  10.8 us
  transfers between devices with their start and end apart: 67, of which 20 were waited for; matrix products, arithmetic and copies ran while one was open for 27% of the time, Pallas kernels for 31%

profile of v2, /device:TPU:0, one launch (start us, length us, event | category | flops | bytes accessed | tf_op | source)
XLA Modules:
  0.0 486.5 jit_solution(3804147832491168755)
XLA Ops:
  0.7 5.6 %concatenate.30 = bf16[3072]{0:T(1024)(128)(2,1)S(1)} concatenate(bf16[192]{0:T(256)(128)(2,1)} %param.18, bf16[192]{0:T(256)(128)(2,1)} %param.19, bf16[192]{0:T(256)(128)(2,1)} %param.20, bf16[192]{0:T(256)(128)(2,1)} %param.21, bf16[576]{0:T(1024)(128)(2,1)} %param.23, bf16[192]{0:T(256)(128)(2,1)} %param.25, bf16[768]{0:T(1024)(128)(2,1)} %param.27, bf16[192]{0:T(256)(128)(2,1)} %param.29, ...), dimensions={0} | concatenate | bytes 12288 | tf_op jit(solution)/shard_map/concatenate | solution.py:96
  6.2 5.1 %collective-permute-start.2 = (bf16[24,128]{1,0:T(8,128)(2,1)S(1)}, bf16[24,128]{1,0:T(8,128)(2,1)}, u32[]{:S(2)}, u32[]{:S(2)}) collective-permute-start(bf16[24,128]{1,0:T(8,128)(2,1)S(1)} %bitcast.253), channel_id=1, source_target_pairs={{0,3},{1,2},{2,1},{3,0},{4,7},{5,6},{6,5},{7,4},{8,11},{9,10},{10,... | collective-permute-start | bytes 18440 | tf_op jit(solution)/shard_map/ppermute | solution.py:30
  23.8 7.1 %slice_reduce_fusion = (bf16[192,4,384]{2,1,0:T(4,128)(2,1)}, bf16[192,4,384]{2,1,0:T(4,128)(2,1)}) fusion(bf16[192,4,2,384]{3,2,1,0:T(2,128)(2,1)S(1)} %reshape.239), kind=kLoop, calls=%fused_computation.27 | loop fusion | bytes 2359296 | tf_op jit(solution)/shard_map/slice | solution.py:518
  34.7 3.2 fusion.9
  49.1 3.8 collective-permute-done.8
  54.4 4.1 collective-permute-done.7
  65.0 3.8 copy.82
  73.9 2.5 collective-permute-start.11
  76.4 2.9 collective-permute-start.10
  79.2 3.1 collective-permute-done.22
  90.3 3.0 collective-permute-start.14
  94.1 7.0 %collective-permute-done.18 = bf16[3,192,384]{2,1,0:T(8,128)(2,1)S(1)} collective-permute-done((bf16[3,192,384]{2,1,0:T(8,128)(2,1)}, bf16[3,192,384]{2,1,0:T(8,128)(2,1)S(1)}, u32[]{:S(2)}, u32[]{:S(2)}) %collective-permute-start.18) | collective-permute-done | bytes 442400 | tf_op jit(solution)/shard_map/ppermute | solution.py:30
  101.1 2.6 pad_maximum_fusion.3.refs_2_
  103.8 6.6 %collective-permute-done.13 = bf16[3,192,384]{2,1,0:T(8,128)(2,1)S(1)} collective-permute-done((bf16[3,192,384]{2,1,0:T(8,128)(2,1)S(1)}, bf16[3,192,384]{2,1,0:T(8,128)(2,1)S(1)}, u32[]{:S(2)}, u32[]{:S(2)}) %collective-permute-start.13) | collective-permute-done | bytes 442400 | tf_op jit(solution)/shard_map/ppermute | solution.py:30
  110.4 7.0 %collective-permute-done.14 = bf16[3,192,384]{2,1,0:T(8,128)(2,1)S(1)} collective-permute-done((bf16[3,192,384]{2,1,0:T(8,128)(2,1)S(1)}, bf16[3,192,384]{2,1,0:T(8,128)(2,1)S(1)}, u32[]{:S(2)}, u32[]{:S(2)}) %collective-permute-start.14) | collective-permute-done | bytes 442400 | tf_op jit(solution)/shard_map/ppermute | solution.py:30
  129.9 3.5 add_convert_fusion
  133.4 2.6 copy.80.x_ref
  136.0 2.6 copy.77.x_ref
  143.8 10.8 %qkv.1.q_ref.k_ref.v_ref = bf16[1024,2304]{1,0:T(8,128)(2,1)S(1)} custom-call(bf16[1024,768]{1,0:T(8,128)(2,1)S(1)} %copy-done.2, bf16[768,2304]{1,0:T(8,128)(2,1)S(1)} %get-tuple-element.47.w_ref, f32[1,2304]{1,0:T(1,128)S(1)} %reshape.250.bias_ref, f32[1024,128]{1,0:T(8,128)S(1)} %copy-done.5, f32[1024,128]{1,0:T(8,128)S(1)} %copy-done.4, ...), custom_call_target="tpu_custom_call" | custom-call | tf_op jit(solution)/shard_map/qkv/pallas_call | solution.py:203
  156.9 55.2 %attention.1 = (bf16[1024,768]{1,0:T(8,128)(2,1)}, bf16[3,1024,768]{2,1,0:T(8,128)(2,1)}) custom-call(bf16[1024,2304]{1,0:T(8,128)(2,1)} %copy-done, bf16[1024,2304]{1,0:T(8,128)(2,1)} %copy-done, bf16[1024,2304]{1,0:T(8,128)(2,1)} %copy-done, bf16[1024,768]{1,0:T(8,128)(2,1)} %get-tuple-element.123.cot_ref, bf16[768,768]{1,0:T(8,128)(2,1)} %copy-done.16, ...), custom_call_target="tpu_custom_call" | custom-call | tf_op jit(solution)/shard_map/attention/pallas_call | solution.py:280
  212.1 20.9 %qkv_grad.1 = (bf16[2,4,4,192,384]{4,3,2,1,0:T(8,128)(2,1)}, f32[1,2304]{1,0:T(1,128)}, f32[1024,768]{1,0:T(8,128)}) custom-call(bf16[3,1024,768]{2,1,0:T(8,128)(2,1)} %get-tuple-element.53.grad_ref, bf16[768,1024]{1,0:T(8,128)(2,1)} %bitcast.204, bf16[768,2304]{1,0:T(8,128)(2,1)} %copy-done.1, bf16[1024,768]{1,0:T(8,128)(2,1)} %get-tuple-element.49.mixed_ref, ...), custom_call_target="tpu_custom_call" | custom-call | tf_op jit(solution)/shard_map/qkv_grad/pallas_call | solution.py:339
  233.0 2.7 reduce_sum.116
  235.7 13.7 %copy.81 = f32[1024,768]{0,1:T(8,128)} copy(f32[1024,768]{1,0:T(8,128)} %get-tuple-element.54) | data formatting | bytes 6291456 | tf_op jit(solution)/shard_map/qkv_grad/pallas_call | solution.py:339
  249.5 3.5 dynamic-slice_bitcast_fusion.2
  254.1 5.5 %add_add_fusion.out_in_ref = f32[1024,768]{1,0:T(8,128)} fusion(f32[1024,768]{1,0:T(8,128)} %param.15, bf16[1024,768]{1,0:T(8,128)(2,1)} %get-tuple-element.49.mixed_ref, bf16[768,768]{1,0:T(8,128)(2,1)S(1)} %copy-done.17, f32[768]{0:T(1024)S(1)} %copy-done.57, f32[768]{0:T(1024)S(1)} %copy-done.56), kind=kOutput, calls=%fused_computation.12 | convolution fusion | flops 1210318848 | bytes 9050112 | tf_op jit(solution)/shard_map/dot_general | solution.py:540
  266.7 27.7 %mlp.2 = (f32[1024,768]{1,0:T(8,128)}, f32[1024,768]{1,0:T(8,128)}, bf16[2,4,4,192,384]{4,3,2,1,0:T(8,128)(2,1)}, f32[1,1536]{1,0:T(1,128)}) custom-call(bf16[1024,768]{1,0:T(8,128)(2,1)} %copy.80.x_ref, bf16[768,1024]{1,0:T(8,128)(2,1)} %bitcast.202, bf16[1024,768]{1,0:T(8,128)(2,1)} %get-tuple-element.123.cot_ref, ...), custom_call_target="tpu_custom_call", output_to_operand_aliasing={{0}: (6, {}), {1}: (7, {})} | custom-call | tf_op jit(solution)/shard_map/mlp/pallas_call | solution.py:402
  294.4 3.5 dynamic-slice_bitcast_fusion.1
  302.7 27.6 %mlp.3 = (f32[1024,768]{1,0:T(8,128)}, f32[1024,768]{1,0:T(8,128)}, bf16[2,4,4,192,384]{4,3,2,1,0:T(8,128)(2,1)}, f32[1,1536]{1,0:T(1,128)}) custom-call(bf16[1024,768]{1,0:T(8,128)(2,1)} %copy.80.x_ref, bf16[768,1024]{1,0:T(8,128)(2,1)} %bitcast.203, bf16[1024,768]{1,0:T(8,128)(2,1)} %get-tuple-element.123.cot_ref, ...), custom_call_target="tpu_custom_call", output_to_operand_aliasing={{0}: (6, {}), {1}: (7, {})} | custom-call | tf_op jit(solution)/shard_map/mlp/pallas_call | solution.py:402
  330.4 3.8 copy.83
  334.2 4.1 multiply_reduce_fusion
  343.8 2.4 collective-permute-start.27
  348.7 2.5 collective-permute-done.25
  351.8 3.2 fusion.2
  357.9 2.5 fusion.1
  365.2 6.9 %collective-permute-done.34 = bf16[2,2,192,384]{3,2,0,1:T(8,128)(2,1)S(1)} collective-permute-done((bf16[2,2,192,384]{3,2,0,1:T(8,128)(2,1)S(1)}, bf16[2,2,192,384]{3,2,0,1:T(8,128)(2,1)S(1)}, u32[]{:S(2)}, u32[]{:S(2)}) %collective-permute-start.34) | collective-permute-done | bytes 589856 | tf_op jit(solution)/shard_map/ppermute | solution.py:30
  374.6 10.1 %collective-permute-done.46 = bf16[2,2,192,384]{3,2,0,1:T(8,128)(2,1)S(1)} collective-permute-done((bf16[2,2,192,384]{3,2,0,1:T(8,128)(2,1)S(1)}, bf16[2,2,192,384]{3,2,0,1:T(8,128)(2,1)S(1)}, u32[]{:S(2)}, u32[]{:S(2)}) %collective-permute-start.46) | collective-permute-done | bytes 589856 | tf_op jit(solution)/shard_map/ppermute | solution.py:30
  387.2 17.0 %collective-permute-done.35 = bf16[2,192,384]{2,1,0:T(8,128)(2,1)S(1)} collective-permute-done((bf16[2,192,384]{2,1,0:T(8,128)(2,1)S(1)}, bf16[2,192,384]{2,1,0:T(8,128)(2,1)S(1)}, u32[]{:S(2)}, u32[]{:S(2)}) %collective-permute-start.35) | collective-permute-done | bytes 294944 | tf_op jit(solution)/shard_map/ppermute | solution.py:30
  406.7 3.4 collective-permute-start.37
  428.0 2.5 collective-permute-start.60
  430.5 5.3 %collective-permute-done.49 = bf16[192,384]{1,0:T(8,128)(2,1)S(1)} collective-permute-done((bf16[192,384]{1,0:T(8,128)(2,1)S(1)}, bf16[192,384]{1,0:T(8,128)(2,1)S(1)}, u32[]{:S(2)}, u32[]{:S(2)}) %collective-permute-start.49) | collective-permute-done | bytes 147488 | tf_op jit(solution)/shard_map/ppermute | solution.py:30
  435.8 2.9 collective-permute-start.62
  440.4 4.9 %collective-permute-done.61 = bf16[192,384]{1,0:T(8,128)(2,1)S(1)} collective-permute-done((bf16[192,384]{1,0:T(8,128)(2,1)S(1)}, bf16[192,384]{1,0:T(8,128)(2,1)S(1)}, u32[]{:S(2)}, u32[]{:S(2)}) %collective-permute-start.61) | collective-permute-done | bytes 147488 | tf_op jit(solution)/shard_map/ppermute | solution.py:30
  446.5 2.6 collective-permute-start.65
  451.9 3.1 collective-permute-start.29
  456.8 3.4 multiply_add_fusion
  460.2 3.5 copy.98
  476.5 3.2 copy.97
  479.8 4.2 reshape.244
  (371 shorter events, 145.5 us)
Async XLA Ops:
  6.2 56.2 %collective-permute-start.2 = (bf16[24,128]{1,0:T(8,128)(2,1)S(1)}, bf16[24,128]{1,0:T(8,128)(2,1)}, u32[]{:S(2)}, u32[]{:S(2)}) collective-permute-start(bf16[24,128]{1,0:T(8,128)(2,1)S(1)} %bitcast.253), channel_id=1, source_target_pairs={{0,3},{1,2},{2,1},{3,0},{4,7},{5,6},{6,5},{7,4},{8,11},{9,10},{10,... | collective-permute-start | bytes 18440 | tf_op jit(solution)/shard_map/ppermute | solution.py:30
  11.3 51.6 %collective-permute-start.1 = (bf16[24,128]{1,0:T(8,128)(2,1)S(1)}, bf16[24,128]{1,0:T(8,128)(2,1)}, u32[]{:S(2)}, u32[]{:S(2)}) collective-permute-start(bf16[24,128]{1,0:T(8,128)(2,1)S(1)} %bitcast.254), channel_id=1, source_target_pairs={{0,2},{1,3},{2,0},{3,1},{4,6},{5,7},{6,4},{7,5},{8,10},{9,11},{10,... | collective-permute-start | bytes 18440 | tf_op jit(solution)/shard_map/ppermute | solution.py:30
  13.6 28.4 %collective-permute-start.5 = (bf16[192,384]{1,0:T(8,128)(2,1)}, bf16[192,384]{1,0:T(8,128)(2,1)}, u32[]{:S(2)}, u32[]{:S(2)}) collective-permute-start(bf16[192,384]{1,0:T(8,128)(2,1)} %pad_maximum_fusion.13), channel_id=1, source_target_pairs={{0,3},{1,2},{2,1},{3,0},{4,7},{5,6},{6,5},{7,4},{8,11},{9,10},{10,... | collective-permute-start | bytes 442376 | tf_op jit(solution)/shard_map/ppermute | solution.py:30
  15.5 26.5 %collective-permute-start.4 = (bf16[192,384]{1,0:T(8,128)(2,1)}, bf16[192,384]{1,0:T(8,128)(2,1)}, u32[]{:S(2)}, u32[]{:S(2)}) collective-permute-start(bf16[192,384]{1,0:T(8,128)(2,1)} %pad_maximum_fusion.13), channel_id=1, source_target_pairs={{0,2},{1,3},{2,0},{3,1},{4,6},{5,7},{6,4},{7,5},{8,10},{9,11},{10,... | collective-permute-start | bytes 442376 | tf_op jit(solution)/shard_map/ppermute | solution.py:30
  16.5 25.5 %collective-permute-start.3 = (bf16[192,384]{1,0:T(8,128)(2,1)}, bf16[192,384]{1,0:T(8,128)(2,1)}, u32[]{:S(2)}, u32[]{:S(2)}) collective-permute-start(bf16[192,384]{1,0:T(8,128)(2,1)} %pad_maximum_fusion.13), channel_id=1, source_target_pairs={{0,1},{1,0},{2,3},{3,2},{4,5},{5,4},{6,7},{7,6},{8,9},{9,8},{10,11... | collective-permute-start | bytes 442376 | tf_op jit(solution)/shard_map/ppermute | solution.py:30
  46.2 12.3 %collective-permute-start.7 = (bf16[192,384]{1,0:T(8,128)(2,1)S(1)}, bf16[192,384]{1,0:T(8,128)(2,1)S(1)}, u32[]{:S(2)}, u32[]{:S(2)}) collective-permute-start(bf16[192,384]{1,0:T(8,128)(2,1)S(1)} %get-tuple-element.41), channel_id=1, source_target_pairs={{0,2},{1,3},{2,0},{3,1},{4,6},{5,7},{6,4},{7,5},{8,10},{9,11},{10,... | collective-permute-start | bytes 442376 | tf_op jit(solution)/shard_map/ppermute | solution.py:30
  46.3 13.6 %collective-permute-start.6 = (bf16[192,384]{1,0:T(8,128)(2,1)S(1)}, bf16[192,384]{1,0:T(8,128)(2,1)S(1)}, u32[]{:S(2)}, u32[]{:S(2)}) collective-permute-start(bf16[192,384]{1,0:T(8,128)(2,1)S(1)} %get-tuple-element.41), channel_id=1, source_target_pairs={{0,1},{1,0},{2,3},{3,2},{4,5},{5,4},{6,7},{7,6},{8,9},{9,8},{10,11... | collective-permute-start | bytes 442376 | tf_op jit(solution)/shard_map/ppermute | solution.py:30
  52.9 21.0 %collective-permute-start.21 = (bf16[3,192,384]{2,1,0:T(8,128)(2,1)}, bf16[3,192,384]{2,1,0:T(8,128)(2,1)}, u32[]{:S(2)}, u32[]{:S(2)}) collective-permute-start(bf16[3,192,384]{2,1,0:T(8,128)(2,1)} %get-tuple-element.157), channel_id=1, source_target_pairs={{0,16},{4,20},{8,24},{12,28},{16,0},{20,4},{24,8},{28,12},{1,17},{... | collective-permute-start | bytes 1327112 | tf_op jit(solution)/shard_map/ppermute | solution.py:30
  58.4 17.9 %collective-permute-start.20 = (bf16[3,192,384]{2,1,0:T(8,128)(2,1)}, bf16[3,192,384]{2,1,0:T(8,128)(2,1)}, u32[]{:S(2)}, u32[]{:S(2)}) collective-permute-start(bf16[3,192,384]{2,1,0:T(8,128)(2,1)} %get-tuple-element.157), channel_id=1, source_target_pairs={{0,8},{4,12},{8,0},{12,4},{16,24},{20,28},{24,16},{28,20},{1,9},{5... | collective-permute-start | bytes 1327112 | tf_op jit(solution)/shard_map/ppermute | solution.py:30
  59.9 22.4 %collective-permute-start.22 = (bf16[3,192,384]{2,1,0:T(8,128)(2,1)}, bf16[3,192,384]{2,1,0:T(8,128)(2,1)}, u32[]{:S(2)}, u32[]{:S(2)}) collective-permute-start(bf16[3,192,384]{2,1,0:T(8,128)(2,1)} %get-tuple-element.157), channel_id=1, source_target_pairs={{0,24},{4,28},{8,16},{12,20},{16,8},{20,12},{24,0},{28,4},{1,25},{... | collective-permute-start | bytes 1327112 | tf_op jit(solution)/shard_map/ppermute | solution.py:30
  62.4 27.0 %collective-permute-start.17 = (bf16[3,192,384]{2,1,0:T(8,128)(2,1)}, bf16[3,192,384]{2,1,0:T(8,128)(2,1)}, u32[]{:S(2)}, u32[]{:S(2)}) collective-permute-start(bf16[3,192,384]{2,1,0:T(8,128)(2,1)} %get-tuple-element.159), channel_id=1, source_target_pairs={{0,16},{4,20},{8,24},{12,28},{16,0},{20,4},{24,8},{28,12},{1,17},{... | collective-permute-start | bytes 1327112 | tf_op jit(solution)/shard_map/ppermute | solution.py:30
  62.9 27.4 %collective-permute-start.16 = (bf16[3,192,384]{2,1,0:T(8,128)(2,1)}, bf16[3,192,384]{2,1,0:T(8,128)(2,1)}, u32[]{:S(2)}, u32[]{:S(2)}) collective-permute-start(bf16[3,192,384]{2,1,0:T(8,128)(2,1)} %get-tuple-element.159), channel_id=1, source_target_pairs={{0,8},{4,12},{8,0},{12,4},{16,24},{20,28},{24,16},{28,20},{1,9},{5... | collective-permute-start | bytes 1327112 | tf_op jit(solution)/shard_map/ppermute | solution.py:30
  73.9 10.2 %collective-permute-start.11 = (bf16[192,384]{1,0:T(8,128)(2,1)S(1)}, bf16[192,384]{1,0:T(8,128)(2,1)S(1)}, u32[]{:S(2)}, u32[]{:S(2)}) collective-permute-start(bf16[192,384]{1,0:T(8,128)(2,1)S(1)} %copy-done.37), channel_id=1, source_target_pairs={{0,3},{1,2},{2,1},{3,0},{4,7},{5,6},{6,5},{7,4},{8,11},{9,10},{10,... | collective-permute-start | bytes 442376 | tf_op jit(solution)/shard_map/ppermute | solution.py:30
  76.4 10.2 %collective-permute-start.10 = (bf16[192,384]{1,0:T(8,128)(2,1)S(1)}, bf16[192,384]{1,0:T(8,128)(2,1)S(1)}, u32[]{:S(2)}, u32[]{:S(2)}) collective-permute-start(bf16[192,384]{1,0:T(8,128)(2,1)S(1)} %copy-done.37), channel_id=1, source_target_pairs={{0,2},{1,3},{2,0},{3,1},{4,6},{5,7},{6,4},{7,5},{8,10},{9,11},{10,... | collective-permute-start | bytes 442376 | tf_op jit(solution)/shard_map/ppermute | solution.py:30
  86.6 14.6 %collective-permute-start.18 = (bf16[3,192,384]{2,1,0:T(8,128)(2,1)}, bf16[3,192,384]{2,1,0:T(8,128)(2,1)S(1)}, u32[]{:S(2)}, u32[]{:S(2)}) collective-permute-start(bf16[3,192,384]{2,1,0:T(8,128)(2,1)} %get-tuple-element.159), channel_id=1, source_target_pairs={{0,24},{4,28},{8,16},{12,20},{16,8},{20,12},{24,0},{28,4},{1,25},{... | collective-permute-start | bytes 1327112 | tf_op jit(solution)/shard_map/ppermute | solution.py:30
  88.1 50.5 %collective-permute-start.23 = (bf16[4,3,192,384]{3,2,1,0:T(8,128)(2,1)S(1)}, bf16[4,3,192,384]{3,2,1,0:T(8,128)(2,1)}, u32[]{:S(2)}, u32[]{:S(2)}) collective-permute-start(bf16[4,3,192,384]{3,2,1,0:T(8,128)(2,1)S(1)} %pad_maximum_fusion.4.refs_2_), channel_id=1, source_target_pairs={{0,4},{4,0},{8,12},{12,8},{16,20},{20,16},{24,28},{28,24},{1,5},{5... | collective-permute-start | bytes 5308424 | tf_op jit(solution)/shard_map/ppermute | solution.py:30
  88.2 22.1 %collective-permute-start.13 = (bf16[3,192,384]{2,1,0:T(8,128)(2,1)S(1)}, bf16[3,192,384]{2,1,0:T(8,128)(2,1)S(1)}, u32[]{:S(2)}, u32[]{:S(2)}) collective-permute-start(bf16[3,192,384]{2,1,0:T(8,128)(2,1)S(1)} %get-tuple-element.161), channel_id=1, source_target_pairs={{0,16},{4,20},{8,24},{12,28},{16,0},{20,4},{24,8},{28,12},{1,17},{... | collective-permute-start | bytes 1327112 | tf_op jit(solution)/shard_map/ppermute | solution.py:30
  89.4 21.0 %collective-permute-start.12 = (bf16[3,192,384]{2,1,0:T(8,128)(2,1)S(1)}, bf16[3,192,384]{2,1,0:T(8,128)(2,1)S(1)}, u32[]{:S(2)}, u32[]{:S(2)}) collective-permute-start(bf16[3,192,384]{2,1,0:T(8,128)(2,1)S(1)} %get-tuple-element.161), channel_id=1, source_target_pairs={{0,8},{4,12},{8,0},{12,4},{16,24},{20,28},{24,16},{28,20},{1,9},{5... | collective-permute-start | bytes 1327112 | tf_op jit(solution)/shard_map/ppermute | solution.py:30
  90.3 27.1 %collective-permute-start.14 = (bf16[3,192,384]{2,1,0:T(8,128)(2,1)S(1)}, bf16[3,192,384]{2,1,0:T(8,128)(2,1)S(1)}, u32[]{:S(2)}, u32[]{:S(2)}) collective-permute-start(bf16[3,192,384]{2,1,0:T(8,128)(2,1)S(1)} %get-tuple-element.161), channel_id=1, source_target_pairs={{0,24},{4,28},{8,16},{12,20},{16,8},{20,12},{24,0},{28,4},{1,25},{... | collective-permute-start | bytes 1327112 | tf_op jit(solution)/shard_map/ppermute | solution.py:30
  103.8 155.8 %collective-permute-start.19 = (bf16[4,3,192,384]{3,2,1,0:T(8,128)(2,1)}, bf16[4,3,192,384]{3,2,1,0:T(8,128)(2,1)}, u32[]{:S(2)}, u32[]{:S(2)}) collective-permute-start(bf16[4,3,192,384]{3,2,1,0:T(8,128)(2,1)} %pad_maximum_fusion.3.refs_2_), channel_id=1, source_target_pairs={{0,4},{4,0},{8,12},{12,8},{16,20},{20,16},{24,28},{28,24},{1,5},{5... | collective-permute-start | bytes 5308424 | tf_op jit(solution)/shard_map/ppermute | solution.py:30
  117.7 180.3 %collective-permute-start.15 = (bf16[4,3,192,384]{3,2,1,0:T(8,128)(2,1)S(1)}, bf16[4,3,192,384]{3,2,1,0:T(8,128)(2,1)}, u32[]{:S(2)}, u32[]{:S(2)}) collective-permute-start(bf16[4,3,192,384]{3,2,1,0:T(8,128)(2,1)S(1)} %pad_maximum_fusion.2.refs_2_), channel_id=1, source_target_pairs={{0,4},{4,0},{8,12},{12,8},{16,20},{20,16},{24,28},{28,24},{1,5},{5... | collective-permute-start | bytes 5308424 | tf_op jit(solution)/shard_map/ppermute | solution.py:30
  252.9 98.9 %collective-permute-start.31 = (bf16[4,4,192,384]{3,2,1,0:T(8,128)(2,1)}, bf16[4,4,192,384]{3,2,1,0:T(8,128)(2,1)}, u32[]{:S(2)}, u32[]{:S(2)}) collective-permute-start(bf16[4,4,192,384]{3,2,1,0:T(8,128)(2,1)} %dynamic-slice_bitcast_fusion.2), channel_id=1, source_target_pairs={{0,4},{4,0},{8,12},{12,8},{16,20},{20,16},{24,28},{28,24},{1,5},{5... | collective-permute-start | bytes 7077896 | tf_op jit(solution)/shard_map/ppermute | solution.py:30
  297.9 59.9 %collective-permute-start.43 = (bf16[4,4,192,384]{3,2,1,0:T(8,128)(2,1)}, bf16[4,4,192,384]{3,2,1,0:T(8,128)(2,1)}, u32[]{:S(2)}, u32[]{:S(2)}) collective-permute-start(bf16[4,4,192,384]{3,2,1,0:T(8,128)(2,1)} %dynamic-slice_bitcast_fusion.1), channel_id=1, source_target_pairs={{0,4},{4,0},{8,12},{12,8},{16,20},{20,16},{24,28},{28,24},{1,5},{5... | collective-permute-start | bytes 7077896 | tf_op jit(solution)/shard_map/ppermute | solution.py:30
  343.1 20.1 %collective-permute-start.55 = (bf16[4,4,192,384]{3,2,1,0:T(8,128)(2,1)S(1)}, bf16[4,4,192,384]{3,2,1,0:T(8,128)(2,1)S(1)}, u32[]{:S(2)}, u32[]{:S(2)}) collective-permute-start(bf16[4,4,192,384]{3,2,1,0:T(8,128)(2,1)S(1)} %dynamic-slice_bitcast_fusion), channel_id=1, source_target_pairs={{0,4},{4,0},{8,12},{12,8},{16,20},{20,16},{24,28},{28,24},{1,5},{5... | collective-permute-start | bytes 7077896 | tf_op jit(solution)/shard_map/ppermute | solution.py:30
  355.8 16.3 %collective-permute-start.34 = (bf16[2,2,192,384]{3,2,0,1:T(8,128)(2,1)S(1)}, bf16[2,2,192,384]{3,2,0,1:T(8,128)(2,1)S(1)}, u32[]{:S(2)}, u32[]{:S(2)}) collective-permute-start(bf16[2,2,192,384]{3,2,0,1:T(8,128)(2,1)S(1)} %dynamic-slice_bitcast_fusion.5), channel_id=1, source_target_pairs={{0,16},{4,20},{8,24},{12,28},{16,0},{20,4},{24,8},{28,12},{1,17},{... | collective-permute-start | bytes 1769480 | tf_op jit(solution)/shard_map/ppermute | solution.py:30
  356.3 17.4 %collective-permute-start.32 = (bf16[2,2,192,384]{3,2,0,1:T(8,128)(2,1)S(1)}, bf16[2,2,192,384]{3,2,0,1:T(8,128)(2,1)S(1)}, u32[]{:S(2)}, u32[]{:S(2)}) collective-permute-start(bf16[2,2,192,384]{3,2,0,1:T(8,128)(2,1)S(1)} %bitcast.224), channel_id=1, source_target_pairs={{0,8},{4,12},{8,0},{12,4},{16,24},{20,28},{24,16},{28,20},{1,9},{5... | collective-permute-start | bytes 1769480 | tf_op jit(solution)/shard_map/ppermute | solution.py:30
  361.1 23.7 %collective-permute-start.46 = (bf16[2,2,192,384]{3,2,0,1:T(8,128)(2,1)S(1)}, bf16[2,2,192,384]{3,2,0,1:T(8,128)(2,1)S(1)}, u32[]{:S(2)}, u32[]{:S(2)}) collective-permute-start(bf16[2,2,192,384]{3,2,0,1:T(8,128)(2,1)S(1)} %dynamic-slice_bitcast_fusion.4), channel_id=1, source_target_pairs={{0,16},{4,20},{8,24},{12,28},{16,0},{20,4},{24,8},{28,12},{1,17},{... | collective-permute-start | bytes 1769480 | tf_op jit(solution)/shard_map/ppermute | solution.py:30
  362.7 22.8 %collective-permute-start.44 = (bf16[2,2,192,384]{3,2,0,1:T(8,128)(2,1)S(1)}, bf16[2,2,192,384]{3,2,0,1:T(8,128)(2,1)S(1)}, u32[]{:S(2)}, u32[]{:S(2)}) collective-permute-start(bf16[2,2,192,384]{3,2,0,1:T(8,128)(2,1)S(1)} %bitcast.225), channel_id=1, source_target_pairs={{0,8},{4,12},{8,0},{12,4},{16,24},{20,28},{24,16},{28,20},{1,9},{5... | collective-permute-start | bytes 1769480 | tf_op jit(solution)/shard_map/ppermute | solution.py:30
  364.6 42.1 %collective-permute-start.58 = (bf16[2,2,192,384]{3,2,0,1:T(8,128)(2,1)S(1)}, bf16[2,2,192,384]{3,2,0,1:T(8,128)(2,1)S(1)}, u32[]{:S(2)}, u32[]{:S(2)}) collective-permute-start(bf16[2,2,192,384]{3,2,0,1:T(8,128)(2,1)S(1)} %dynamic-slice_bitcast_fusion.3), channel_id=1, source_target_pairs={{0,16},{4,20},{8,24},{12,28},{16,0},{20,4},{24,8},{28,12},{1,17},{... | collective-permute-start | bytes 1769480 | tf_op jit(solution)/shard_map/ppermute | solution.py:30
  372.1 38.2 %collective-permute-start.56 = (bf16[2,2,192,384]{3,2,0,1:T(8,128)(2,1)S(1)}, bf16[2,2,192,384]{3,2,0,1:T(8,128)(2,1)S(1)}, u32[]{:S(2)}, u32[]{:S(2)}) collective-permute-start(bf16[2,2,192,384]{3,2,0,1:T(8,128)(2,1)S(1)} %bitcast.223), channel_id=1, source_target_pairs={{0,8},{4,12},{8,0},{12,4},{16,24},{20,28},{24,16},{28,20},{1,9},{5... | collective-permute-start | bytes 1769480 | tf_op jit(solution)/shard_map/ppermute | solution.py:30
  373.8 30.4 %collective-permute-start.35 = (bf16[2,192,384]{2,1,0:T(8,128)(2,1)S(1)}, bf16[2,192,384]{2,1,0:T(8,128)(2,1)S(1)}, u32[]{:S(2)}, u32[]{:S(2)}) collective-permute-start(bf16[2,192,384]{2,1,0:T(8,128)(2,1)S(1)} %dynamic-slice_bitcast_fusion.10), channel_id=1, source_target_pairs={{0,8},{4,12},{8,0},{12,4},{16,24},{20,28},{24,16},{28,20},{1,9},{5... | collective-permute-start | bytes 884744 | tf_op jit(solution)/shard_map/ppermute | solution.py:30
  384.7 21.1 %collective-permute-start.33 = (bf16[2,192,384]{2,1,0:T(8,128)(2,1)S(1)}, bf16[2,192,384]{2,1,0:T(8,128)(2,1)S(1)}, u32[]{:S(2)}, u32[]{:S(2)}) collective-permute-start(bf16[2,192,384]{2,1,0:T(8,128)(2,1)S(1)} %dynamic-slice_bitcast_fusion.11), channel_id=1, source_target_pairs={{0,16},{4,20},{8,24},{12,28},{16,0},{20,4},{24,8},{28,12},{1,17},{... | collective-permute-start | bytes 884744 | tf_op jit(solution)/shard_map/ppermute | solution.py:30
  385.5 33.8 %collective-permute-start.47 = (bf16[2,192,384]{2,1,0:T(8,128)(2,1)S(1)}, bf16[2,192,384]{2,1,0:T(8,128)(2,1)S(1)}, u32[]{:S(2)}, u32[]{:S(2)}) collective-permute-start(bf16[2,192,384]{2,1,0:T(8,128)(2,1)S(1)} %dynamic-slice_bitcast_fusion.8), channel_id=1, source_target_pairs={{0,8},{4,12},{8,0},{12,4},{16,24},{20,28},{24,16},{28,20},{1,9},{5... | collective-permute-start | bytes 884744 | tf_op jit(solution)/shard_map/ppermute | solution.py:30
  404.2 17.2 %collective-permute-start.45 = (bf16[2,192,384]{2,1,0:T(8,128)(2,1)S(1)}, bf16[2,192,384]{2,1,0:T(8,128)(2,1)S(1)}, u32[]{:S(2)}, u32[]{:S(2)}) collective-permute-start(bf16[2,192,384]{2,1,0:T(8,128)(2,1)S(1)} %dynamic-slice_bitcast_fusion.9), channel_id=1, source_target_pairs={{0,16},{4,20},{8,24},{12,28},{16,0},{20,4},{24,8},{28,12},{1,17},{... | collective-permute-start | bytes 884744 | tf_op jit(solution)/shard_map/ppermute | solution.py:30
  411.3 12.7 %collective-permute-start.59 = (bf16[2,192,384]{2,1,0:T(8,128)(2,1)S(1)}, bf16[2,192,384]{2,1,0:T(8,128)(2,1)S(1)}, u32[]{:S(2)}, u32[]{:S(2)}) collective-permute-start(bf16[2,192,384]{2,1,0:T(8,128)(2,1)S(1)} %dynamic-slice_bitcast_fusion.6), channel_id=1, source_target_pairs={{0,8},{4,12},{8,0},{12,4},{16,24},{20,28},{24,16},{28,20},{1,9},{5... | collective-permute-start | bytes 884744 | tf_op jit(solution)/shard_map/ppermute | solution.py:30
  414.8 11.3 %collective-permute-start.57 = (bf16[2,192,384]{2,1,0:T(8,128)(2,1)S(1)}, bf16[2,192,384]{2,1,0:T(8,128)(2,1)S(1)}, u32[]{:S(2)}, u32[]{:S(2)}) collective-permute-start(bf16[2,192,384]{2,1,0:T(8,128)(2,1)S(1)} %dynamic-slice_bitcast_fusion.7), channel_id=1, source_target_pairs={{0,16},{4,20},{8,24},{12,28},{16,0},{20,4},{24,8},{28,12},{1,17},{... | collective-permute-start | bytes 884744 | tf_op jit(solution)/shard_map/ppermute | solution.py:30
  417.6 21.3 %collective-permute-start.41 = (bf16[192,384]{1,0:T(8,128)(2,1)S(1)}, bf16[192,384]{1,0:T(8,128)(2,1)S(1)}, u32[]{:S(2)}, u32[]{:S(2)}) collective-permute-start(bf16[192,384]{1,0:T(8,128)(2,1)S(1)} %fusion.24), channel_id=1, source_target_pairs={{0,24},{4,28},{8,16},{12,20},{16,8},{20,12},{24,0},{28,4},{1,25},{... | collective-permute-start | bytes 442376 | tf_op jit(solution)/shard_map/ppermute | solution.py:30
  419.2 27.2 %collective-permute-start.40 = (bf16[192,384]{1,0:T(8,128)(2,1)S(1)}, bf16[192,384]{1,0:T(8,128)(2,1)S(1)}, u32[]{:S(2)}, u32[]{:S(2)}) collective-permute-start(bf16[192,384]{1,0:T(8,128)(2,1)S(1)} %fusion.24), channel_id=1, source_target_pairs={{0,16},{4,20},{8,24},{12,28},{16,0},{20,4},{24,8},{28,12},{1,17},{... | collective-permute-start | bytes 442376 | tf_op jit(solution)/shard_map/ppermute | solution.py:30
  424.0 11.8 %collective-permute-start.49 = (bf16[192,384]{1,0:T(8,128)(2,1)S(1)}, bf16[192,384]{1,0:T(8,128)(2,1)S(1)}, u32[]{:S(2)}, u32[]{:S(2)}) collective-permute-start(bf16[192,384]{1,0:T(8,128)(2,1)S(1)} %get-tuple-element.148), channel_id=1, source_target_pairs={{0,2},{1,3},{2,0},{3,1},{4,6},{5,7},{6,4},{7,5},{8,10},{9,11},{10,... | collective-permute-start | bytes 442376 | tf_op jit(solution)/shard_map/ppermute | solution.py:30
  426.1 9.7 %collective-permute-start.50 = (bf16[192,384]{1,0:T(8,128)(2,1)S(1)}, bf16[192,384]{1,0:T(8,128)(2,1)S(1)}, u32[]{:S(2)}, u32[]{:S(2)}) collective-permute-start(bf16[192,384]{1,0:T(8,128)(2,1)S(1)} %get-tuple-element.149), channel_id=1, source_target_pairs={{0,3},{1,2},{2,1},{3,0},{4,7},{5,6},{6,5},{7,4},{8,11},{9,10},{10,... | collective-permute-start | bytes 442376 | tf_op jit(solution)/shard_map/ppermute | solution.py:30
  428.0 11.9 %collective-permute-start.60 = (bf16[192,384]{1,0:T(8,128)(2,1)S(1)}, bf16[192,384]{1,0:T(8,128)(2,1)S(1)}, u32[]{:S(2)}, u32[]{:S(2)}) collective-permute-start(bf16[192,384]{1,0:T(8,128)(2,1)S(1)} %get-tuple-element.150), channel_id=1, source_target_pairs={{0,1},{1,0},{2,3},{3,2},{4,5},{5,4},{6,7},{7,6},{8,9},{9,8},{10,11... | collective-permute-start | bytes 442376 | tf_op jit(solution)/shard_map/ppermute | solution.py:30
  435.8 9.6 %collective-permute-start.61 = (bf16[192,384]{1,0:T(8,128)(2,1)S(1)}, bf16[192,384]{1,0:T(8,128)(2,1)S(1)}, u32[]{:S(2)}, u32[]{:S(2)}) collective-permute-start(bf16[192,384]{1,0:T(8,128)(2,1)S(1)} %get-tuple-element.151), channel_id=1, source_target_pairs={{0,2},{1,3},{2,0},{3,1},{4,6},{5,7},{6,4},{7,5},{8,10},{9,11},{10,... | collective-permute-start | bytes 442376 | tf_op jit(solution)/shard_map/ppermute | solution.py:30
  435.8 9.6 %collective-permute-start.62 = (bf16[192,384]{1,0:T(8,128)(2,1)S(1)}, bf16[192,384]{1,0:T(8,128)(2,1)S(1)}, u32[]{:S(2)}, u32[]{:S(2)}) collective-permute-start(bf16[192,384]{1,0:T(8,128)(2,1)S(1)} %get-tuple-element.152), channel_id=1, source_target_pairs={{0,3},{1,2},{2,1},{3,0},{4,7},{5,6},{6,5},{7,4},{8,11},{9,10},{10,... | collective-permute-start | bytes 442376 | tf_op jit(solution)/shard_map/ppermute | solution.py:30
  438.9 10.2 %collective-permute-start.39 = (bf16[192,384]{1,0:T(8,128)(2,1)S(1)}, bf16[192,384]{1,0:T(8,128)(2,1)S(1)}, u32[]{:S(2)}, u32[]{:S(2)}) collective-permute-start(bf16[192,384]{1,0:T(8,128)(2,1)S(1)} %fusion.24), channel_id=1, source_target_pairs={{0,8},{4,12},{8,0},{12,4},{16,24},{20,28},{24,16},{28,20},{1,9},{5... | collective-permute-start | bytes 442376 | tf_op jit(solution)/shard_map/ppermute | solution.py:30
  451.9 11.8 %collective-permute-start.29 = (f32[72,128]{1,0:T(8,128)}, f32[72,128]{1,0:T(8,128)S(1)}, u32[]{:S(2)}, u32[]{:S(2)}) collective-permute-start(f32[72,128]{1,0:T(8,128)} %add_add_fusion.1), channel_id=1, source_target_pairs={{0,2},{1,3},{2,0},{3,1},{4,6},{5,7},{6,4},{7,5},{8,10},{9,11},{10,... | collective-permute-start | bytes 110600 | tf_op jit(solution)/shard_map/ppermute | solution.py:30
  456.0 10.5 %collective-permute-start.42 = (bf16[4,192,384]{2,1,0:T(8,128)(2,1)S(1)}, bf16[4,192,384]{2,1,0:T(8,128)(2,1)S(1)}, u32[]{:S(2)}, u32[]{:S(2)}) collective-permute-start(bf16[4,192,384]{2,1,0:T(8,128)(2,1)S(1)} %pad_maximum_fusion.5.parts_ref), channel_id=1, source_target_pairs={{0,4},{4,0},{8,12},{12,8},{16,20},{20,16},{24,28},{28,24},{1,5},{5... | collective-permute-start | bytes 1769480 | tf_op jit(solution)/shard_map/ppermute | solution.py:30
  456.0 12.6 %collective-permute-start.54 = (bf16[4,192,384]{2,1,0:T(8,128)(2,1)S(1)}, bf16[4,192,384]{2,1,0:T(8,128)(2,1)S(1)}, u32[]{:S(2)}, u32[]{:S(2)}) collective-permute-start(bf16[4,192,384]{2,1,0:T(8,128)(2,1)S(1)} %pad_maximum_fusion.6.parts_ref), channel_id=1, source_target_pairs={{0,4},{4,0},{8,12},{12,8},{16,20},{20,16},{24,28},{28,24},{1,5},{5... | collective-permute-start | bytes 1769480 | tf_op jit(solution)/shard_map/ppermute | solution.py:30
  456.6 15.1 %collective-permute-start.66 = (bf16[4,192,384]{2,1,0:T(8,128)(2,1)S(1)}, bf16[4,192,384]{2,1,0:T(8,128)(2,1)}, u32[]{:S(2)}, u32[]{:S(2)}) collective-permute-start(bf16[4,192,384]{2,1,0:T(8,128)(2,1)S(1)} %pad_maximum_fusion.7.parts_ref), channel_id=1, source_target_pairs={{0,4},{4,0},{8,12},{12,8},{16,20},{20,16},{24,28},{28,24},{1,5},{5... | collective-permute-start | bytes 1769480 | tf_op jit(solution)/shard_map/ppermute | solution.py:30
  (85 other events, 640.7 us)
